TPU v7x, 32 devices: a whole 2x2x4 slice. The times are simulated.
32 devices in a mesh: groups: 2 (over x), beam: 4 (over z), ctx: 4 (over y, core).
Axes of the slice: x: 2, y: 2, z: 4, core: 2. Of those that a mesh axis runs over, the one named last changes fastest.
Arguments:
- queries: bfloat16 [8, 16384], P(('groups', 'beam'), 'ctx'), parts along dimension 0
- new_keys: bfloat16 [8, 1024], P(('groups', 'beam')), parts along dimension 0, may hold values from -16 to 16
- new_values: bfloat16 [8, 1024], P(('groups', 'beam')), parts along dimension 0, may hold values from -9 to 9
- cache_keys: bfloat16 [8, 2048, 8, 128], P(('groups', 'beam'), 'ctx'), parts along dimension 0
- cache_values: bfloat16 [8, 2048, 8, 128], P(('groups', 'beam'), 'ctx'), parts along dimension 0, may hold values from -6 to 6
- parents: int32 [8], P('groups'), parts along dimension 0, may hold values from 0 to 3
- lengths: int32 [8], P('groups'), parts along dimension 0, may hold values from 8 to 16, as said below
- out_weight: bfloat16 [16384, 16384], P('ctx', 'beam'), may hold values from -0.046875 to 0.046875
Outputs:
- projected: bfloat16 [8, 16384], P('groups', ('beam', 'ctx')), parts along dimension 0
There are 2 independent parts, one for each index of `groups`. A program takes and returns all parts, laid end to end along the dimension named above; an argument that names none is the same for every part. Nothing has to cross between parts.
Inputs may be any that keep to these rules, and one draw needn't show every extreme that they name: `lengths`: each previous beam holds at least half of its 16 spans; in every draw some beam is full.
All inputs are finite; a program needn't handle non-finite values.
Results may differ from a plain program's by a relative error of at most 0.012.
Values may be sent and summed in bfloat16 or wider, within the bound.
No kernel may reach another device: no remote copies, remote signals or barrier semaphores. Data moves between devices by JAX's collectives and lax.ppermute only.
A program may use at most 64 MiB of HBM per device.

v0:
```python
import math

import jax
import jax.numpy as jnp
from jax import lax
from jax.sharding import PartitionSpec as P

H = 128
KVH = 8
HD = 128
SPAN = 128


MASKED = -1e30


def shifted(array, axis, by):
    length = lax.axis_size(axis)
    return lax.ppermute(array, axis, [(i, (i + by) % length) for i in range(length)])


def local_partial(query_block, head_start, keys_here, values_here, usable):
    row_count = query_block.shape[0]
    head_count = query_block.shape[1]
    group_size = H // KVH
    kv_count = max(1, head_count // group_size)
    per_kv = min(head_count, group_size)
    kv_start = head_start // group_size
    key_heads = lax.dynamic_slice_in_dim(keys_here, kv_start, kv_count, 1)
    value_heads = lax.dynamic_slice_in_dim(values_here, kv_start, kv_count, 1)
    grouped = query_block.reshape(row_count, kv_count, per_kv, HD)
    scores = jnp.einsum("rkgd,tkd->rkgt", grouped, key_heads, preferred_element_type=jnp.float32)
    scores = scores * (1.0 / math.sqrt(HD))
    usable_mask = usable[:, None, None, :]
    scores = jnp.where(usable_mask, scores, MASKED)
    peak = jnp.max(scores, axis=-1)
    weights = jnp.where(usable_mask, jnp.exp(scores - peak[..., None]), 0.0)
    weight_sum = jnp.sum(weights, axis=-1)
    blended = jnp.einsum(
        "rkgt,tkd->rkgd",
        weights.astype(jnp.bfloat16),
        value_heads,
        preferred_element_type=jnp.float32,
    )
    return (
        peak.reshape(row_count, head_count),
        weight_sum.reshape(row_count, head_count),
        blended.reshape(row_count, head_count, HD),
    )


def own_token(query_block, head_start, key_rows, value_rows):
    row_count = query_block.shape[0]
    head_count = query_block.shape[1]
    group_size = H // KVH
    kv_count = max(1, head_count // group_size)
    per_kv = min(head_count, group_size)
    kv_start = head_start // group_size
    key_heads = lax.dynamic_slice_in_dim(
        key_rows.reshape(row_count, KVH, HD), kv_start, kv_count, 1
    )
    value_heads = lax.dynamic_slice_in_dim(
        value_rows.reshape(row_count, KVH, HD), kv_start, kv_count, 1
    )
    grouped = query_block.reshape(row_count, kv_count, per_kv, HD)
    own_score = jnp.einsum("rkgd,rkd->rkg", grouped, key_heads, preferred_element_type=jnp.float32)
    own_score = own_score * (1.0 / math.sqrt(HD))
    blended = jnp.broadcast_to(
        value_heads.astype(jnp.float32)[:, :, None, :], (row_count, kv_count, per_kv, HD)
    )
    return (
        own_score.reshape(row_count, head_count),
        jnp.ones((row_count, head_count), jnp.float32),
        blended.reshape(row_count, head_count, HD),
    )


def combine(earlier, later):
    peak = jnp.maximum(earlier[0], later[0])
    early_scale = jnp.exp(earlier[0] - peak)
    late_scale = jnp.exp(later[0] - peak)
    weight_sum = earlier[1] * early_scale + later[1] * late_scale
    blended = earlier[2] * early_scale[..., None] + later[2] * late_scale[..., None]
    return (peak, weight_sum, blended)


def per_device(
    queries, new_keys, new_values, cache_keys, cache_values, parents, lengths, out_weight
):
    ctx_count = lax.axis_size("ctx")
    ctx_index = lax.axis_index("ctx")
    beam_index = lax.axis_index("beam")
    local_tokens = cache_keys.shape[1]
    head_share = queries.shape[1] // HD
    row_query, row_key, row_value = (
        lax.all_gather(queries, "beam", axis=0, tiled=True),
        lax.all_gather(new_keys, "beam", axis=0, tiled=True),
        lax.all_gather(new_values, "beam", axis=0, tiled=True),
    )
    keys_here = cache_keys[0]
    values_here = cache_values[0]
    row_length = jnp.broadcast_to(lengths[beam_index], (row_query.shape[0],))
    row_keep = (parents == beam_index).astype(jnp.float32)
    row_count = row_query.shape[0]
    positions = ctx_index * local_tokens + jnp.arange(local_tokens, dtype=jnp.int32)
    usable = positions[None, :] < (row_length * SPAN)[:, None]
    home_start = ctx_index * head_share
    blocks = row_query.reshape(row_count, head_share, HD)
    home_state = own_token(blocks, home_start, row_key, row_value)

    def visit(visit_step, packet):
        anchor = (ctx_index - visit_step) % ctx_count
        partial_state = local_partial(
            packet[0], anchor * head_share, keys_here, values_here, usable
        )
        updated = combine((packet[1], packet[2], packet[3]), partial_state)
        moved_rows = shifted(packet[0], "ctx", 1)
        moved_state = shifted((updated[0], updated[1], updated[2]), "ctx", 1)
        return (moved_rows, moved_state[0], moved_state[1], moved_state[2])

    packet = lax.fori_loop(0, ctx_count, visit, (blocks,) + home_state)
    weight_sum = packet[2]
    blended = packet[3]
    result = (blended / weight_sum[..., None]).reshape(row_count, head_share * HD) * row_keep[
        :, None
    ]
    attended = lax.psum_scatter(result, "beam", scatter_dimension=0, tiled=True).astype(
        jnp.bfloat16
    )
    all_beams = lax.all_gather(attended, "beam", axis=0, tiled=True)
    partial_out = jnp.dot(all_beams, out_weight, preferred_element_type=jnp.float32)
    return lax.psum_scatter(partial_out, "ctx", scatter_dimension=1, tiled=True).astype(
        jnp.bfloat16
    )


def solution(mesh):
    placed = (
        P(("groups", "beam"), "ctx"),
        P(("groups", "beam"), None),
        P(("groups", "beam"), None),
        P(("groups", "beam"), "ctx", None, None),
        P(("groups", "beam"), "ctx", None, None),
        P("groups"),
        P("groups"),
        P("ctx", "beam"),
    )
    return jax.shard_map(
        per_device,
        mesh=mesh,
        in_specs=placed,
        out_specs=P("groups", ("beam", "ctx")),
        check_vma=False,
    )
```

profile of v0, /device:TPU:0, one launch (start us, length us, event | category | flops | bytes accessed | tf_op | source)
XLA Modules:
  0.0 166.1 jit_solution(13171231495237748360)
XLA Ops:
  6.5 0.7 compare_convert_fusion
  7.2 15.0 %all-gather.1 = bf16[4,1,1024]{2,1,0:T(2,128)(2,1)S(1)} all-gather(bf16[1,1,1024]{2,1,0:T(2,128)(2,1)} %bitcast.86), channel_id=1, replica_groups=mesh['groups'=2,'beam'=4,'ctx'=4] {'beam'}, dimensions={0}, use_global_device_ids=true | all-gather | bytes 10240 | tf_op jit(solution)/shard_map/all_gather | solution.py:97
  22.3 13.4 %all-gather.2 = bf16[4,1,1024]{2,1,0:T(2,128)(2,1)S(1)} all-gather(bf16[1,1,1024]{2,1,0:T(2,128)(2,1)} %bitcast.87), channel_id=1, replica_groups=mesh['groups'=2,'beam'=4,'ctx'=4] {'beam'}, dimensions={0}, use_global_device_ids=true | all-gather | bytes 10240 | tf_op jit(solution)/shard_map/all_gather | solution.py:98
  35.8 13.4 %all-gather = bf16[4,1,4096]{2,1,0:T(2,128)(2,1)S(1)} all-gather(bf16[1,1,4096]{2,1,0:T(2,128)(2,1)} %bitcast.83), channel_id=1, replica_groups=mesh['groups'=2,'beam'=4,'ctx'=4] {'beam'}, dimensions={0}, use_global_device_ids=true | all-gather | bytes 40960 | tf_op jit(solution)/shard_map/all_gather | solution.py:96
  49.6 1.2 dynamic_slice.31
  51.4 1.9 %copy_bitcast_fusion = (bf16[512,8,128]{2,0,1:T(8,128)(2,1)S(1)}, bf16[512,8,128]{2,0,1:T(8,128)(2,1)S(1)}) fusion(bf16[1,512,8,128]{3,2,1,0:T(8,128)(2,1)} %param.14, bf16[1,512,8,128]{3,2,1,0:T(8,128)(2,1)} %param.13), kind=kLoop, calls=%fused_computation.25 | loop fusion | bytes 4194304 | tf_op jit(solution)/shard_map/squeeze | solution.py:101
  53.4 21.8 %while.22 = (s32[]{:T(128)}, bf16[4,32,128]{2,1,0:T(8,128)(2,1)S(1)}, f32[4,32]{1,0:T(4,128)S(1)}, f32[4,32]{1,0:T(4,128)S(1)}, f32[4,32,128]{2,1,0:T(8,128)S(1)...) while((s32[]{:T(128)}, ...), condition=%wide.region_3.4_spmd.clone, body=%wide.region_0.3_spmd.clone.sunk | while | flops 34193952 | bytes 2216578 | solution.py:121
  53.4 0.3 fusion.35
  53.9 0.2 convolution_bitcast_fusion.3
  54.5 1.6 collective-permute-start
  56.2 0.6 collective-permute-start.2
  56.8 2.4 %collective-permute-done.1 = f32[4,32]{1,0:T(4,128)S(1)} collective-permute-done((f32[4,32]{1,0:T(4,128)S(1)}, f32[4,32]{1,0:T(4,128)S(1)}, u32[]{:S(2)}, u32[]{:S(2)}) %collective-permute-start.1) | collective-permute-done | bytes 544 | tf_op jit(solution)/shard_map/while/body/eval_jaxpr/ppermute | solution.py:19
  59.3 0.3 fusion.35
  59.8 0.2 convolution_bitcast_fusion.3
  60.4 1.0 collective-permute-start
  61.5 1.1 collective-permute-start.2
  62.6 1.8 %collective-permute-done.1 = f32[4,32]{1,0:T(4,128)S(1)} collective-permute-done((f32[4,32]{1,0:T(4,128)S(1)}, f32[4,32]{1,0:T(4,128)S(1)}, u32[]{:S(2)}, u32[]{:S(2)}) %collective-permute-start.1) | collective-permute-done | bytes 544 | tf_op jit(solution)/shard_map/while/body/eval_jaxpr/ppermute | solution.py:19
  64.5 0.3 fusion.35
  65.6 1.2 collective-permute-start
  66.9 1.0 collective-permute-start.2
  67.9 2.0 %collective-permute-done.1 = f32[4,32]{1,0:T(4,128)S(1)} collective-permute-done((f32[4,32]{1,0:T(4,128)S(1)}, f32[4,32]{1,0:T(4,128)S(1)}, u32[]{:S(2)}, u32[]{:S(2)}) %collective-permute-start.1) | collective-permute-done | bytes 544 | tf_op jit(solution)/shard_map/while/body/eval_jaxpr/ppermute | solution.py:19
  69.9 0.3 fusion.35
  71.1 1.0 collective-permute-start
  72.2 1.1 collective-permute-start.2
  73.3 1.8 %collective-permute-done.1 = f32[4,32]{1,0:T(4,128)S(1)} collective-permute-done((f32[4,32]{1,0:T(4,128)S(1)}, f32[4,32]{1,0:T(4,128)S(1)}, u32[]{:S(2)}, u32[]{:S(2)}) %collective-permute-start.1) | collective-permute-done | bytes 544 | tf_op jit(solution)/shard_map/while/body/eval_jaxpr/ppermute | solution.py:19
  75.4 19.6 %all-reduce = bf16[4,4096]{1,0:T(4,128)(2,1)S(1)} all-reduce(f32[4,4096]{1,0:T(4,128)S(1)} %bitcast_multiply_fusion.1), channel_id=2, replica_groups=mesh['groups'=2,'beam'=4,'ctx'=4] {'beam'}, use_global_device_ids=true, to_apply=%region_4.5.clone | all-reduce | flops 16384 | bytes 98304
  95.0 1.2 dynamic-slice
  96.2 0.7 fusion.21
  96.9 13.1 %all-gather.3 = bf16[4,1,4096]{2,1,0:T(2,128)(2,1)S(1)} all-gather(bf16[1,1,4096]{2,1,0:T(2,128)(2,1)S(1)} %fusion.21), channel_id=1, replica_groups=mesh['groups'=2,'beam'=4,'ctx'=4] {'beam'}, dimensions={0}, use_global_device_ids=true | all-gather | bytes 40960 | tf_op jit(solution)/shard_map/all_gather | solution.py:130
  110.0 18.2 %convolution_bitcast_fusion.1 = f32[4096,4]{1,0:T(8,128)} fusion(bf16[4096,4096]{1,0:T(8,128)(2,1)} %param.17, bf16[4,1,4096]{2,1,0:T(2,128)(2,1)S(1)} %all-gather.3), kind=kOutput, calls=%fused_computation.24 | convolution fusion | flops 134217728 | bytes 33652736
  128.3 29.1 %reduce-scatter.4.cloned.1.call-done = f32[1024,4]{1,0:T(8,128)} async-done(((f32[4096,4]{1,0:T(8,128)}), f32[1024,4]{1,0:T(8,128)}) %reduce-scatter.4.cloned.1.call-update) | async-done | bytes 16400
  157.4 1.8 %copy.35 = bf16[4,1024]{1,0:T(4,128)(2,1)} copy(f32[4,1024]{0,1:T(8,128)} %bitcast.79) | data formatting | bytes 24576
  (76 shorter events, 4.0 us)
Async XLA Ops:
  6.5 150.9 %reduce-scatter.4.cloned.1.call-start = ((), (), s32[]{:S(2)}) async-start(), calls=%async_computation.1 | async-start | bytes 2621440
  54.5 4.8 %collective-permute-start.3 = (f32[4,32,128]{2,1,0:T(8,128)S(1)}, f32[4,32,128]{2,1,0:T(8,128)S(1)}, u32[]{:S(2)}, u32[]{:S(2)}) collective-permute-start(f32[4,32,128]{2,1,0:T(8,128)S(1)} %fusion.37), channel_id=1, source_target_pairs={{0,1},{1,2},{2,3},{3,0},{4,5},{5,6},{6,7},{7,4},{8,9},{9,10},{10,1... | collective-permute-start | bytes 196616 | tf_op jit(solution)/shard_map/while/body/eval_jaxpr/ppermute | solution.py:19
  54.5 4.7 %collective-permute-start = (bf16[4,32,128]{2,1,0:T(8,128)(2,1)S(1)}, bf16[4,32,128]{2,1,0:T(8,128)(2,1)S(1)}, u32[]{:S(2)}, u32[]{:S(2)}) collective-permute-start(bf16[4,32,128]{2,1,0:T(8,128)(2,1)S(1)} %copy.76), channel_id=1, source_target_pairs={{0,1},{1,2},{2,3},{3,0},{4,5},{5,6},{6,7},{7,4},{8,9},{9,10},{10,1... | collective-permute-start | bytes 98312 | tf_op jit(solution)/shard_map/while/body/eval_jaxpr/ppermute | solution.py:19
  56.2 3.0 %collective-permute-start.1 = (f32[4,32]{1,0:T(4,128)S(1)}, f32[4,32]{1,0:T(4,128)S(1)}, u32[]{:S(2)}, u32[]{:S(2)}) collective-permute-start(f32[4,32]{1,0:T(4,128)S(1)} %get-tuple-element.343), channel_id=1, source_target_pairs={{0,1},{1,2},{2,3},{3,0},{4,5},{5,6},{6,7},{7,4},{8,9},{9,10},{10,1... | collective-permute-start | bytes 1544 | tf_op jit(solution)/shard_map/while/body/eval_jaxpr/ppermute | solution.py:19
  56.2 3.0 %collective-permute-start.2 = (f32[4,32]{1,0:T(4,128)S(1)}, f32[4,32]{1,0:T(4,128)S(1)}, u32[]{:S(2)}, u32[]{:S(2)}) collective-permute-start(f32[4,32]{1,0:T(4,128)S(1)} %get-tuple-element.344), channel_id=1, source_target_pairs={{0,1},{1,2},{2,3},{3,0},{4,5},{5,6},{6,7},{7,4},{8,9},{9,10},{10,1... | collective-permute-start | bytes 1544 | tf_op jit(solution)/shard_map/while/body/eval_jaxpr/ppermute | solution.py:19
  60.3 4.2 %collective-permute-start.3 = (f32[4,32,128]{2,1,0:T(8,128)S(1)}, f32[4,32,128]{2,1,0:T(8,128)S(1)}, u32[]{:S(2)}, u32[]{:S(2)}) collective-permute-start(f32[4,32,128]{2,1,0:T(8,128)S(1)} %fusion.37), channel_id=1, source_target_pairs={{0,1},{1,2},{2,3},{3,0},{4,5},{5,6},{6,7},{7,4},{8,9},{9,10},{10,1... | collective-permute-start | bytes 196616 | tf_op jit(solution)/shard_map/while/body/eval_jaxpr/ppermute | solution.py:19
  60.4 4.1 %collective-permute-start = (bf16[4,32,128]{2,1,0:T(8,128)(2,1)S(1)}, bf16[4,32,128]{2,1,0:T(8,128)(2,1)S(1)}, u32[]{:S(2)}, u32[]{:S(2)}) collective-permute-start(bf16[4,32,128]{2,1,0:T(8,128)(2,1)S(1)} %copy.76), channel_id=1, source_target_pairs={{0,1},{1,2},{2,3},{3,0},{4,5},{5,6},{6,7},{7,4},{8,9},{9,10},{10,1... | collective-permute-start | bytes 98312 | tf_op jit(solution)/shard_map/while/body/eval_jaxpr/ppermute | solution.py:19
  61.4 3.0 %collective-permute-start.1 = (f32[4,32]{1,0:T(4,128)S(1)}, f32[4,32]{1,0:T(4,128)S(1)}, u32[]{:S(2)}, u32[]{:S(2)}) collective-permute-start(f32[4,32]{1,0:T(4,128)S(1)} %get-tuple-element.343), channel_id=1, source_target_pairs={{0,1},{1,2},{2,3},{3,0},{4,5},{5,6},{6,7},{7,4},{8,9},{9,10},{10,1... | collective-permute-start | bytes 1544 | tf_op jit(solution)/shard_map/while/body/eval_jaxpr/ppermute | solution.py:19
  61.5 3.0 %collective-permute-start.2 = (f32[4,32]{1,0:T(4,128)S(1)}, f32[4,32]{1,0:T(4,128)S(1)}, u32[]{:S(2)}, u32[]{:S(2)}) collective-permute-start(f32[4,32]{1,0:T(4,128)S(1)} %get-tuple-element.344), channel_id=1, source_target_pairs={{0,1},{1,2},{2,3},{3,0},{4,5},{5,6},{6,7},{7,4},{8,9},{9,10},{10,1... | collective-permute-start | bytes 1544 | tf_op jit(solution)/shard_map/while/body/eval_jaxpr/ppermute | solution.py:19
  65.6 4.3 %collective-permute-start.3 = (f32[4,32,128]{2,1,0:T(8,128)S(1)}, f32[4,32,128]{2,1,0:T(8,128)S(1)}, u32[]{:S(2)}, u32[]{:S(2)}) collective-permute-start(f32[4,32,128]{2,1,0:T(8,128)S(1)} %fusion.37), channel_id=1, source_target_pairs={{0,1},{1,2},{2,3},{3,0},{4,5},{5,6},{6,7},{7,4},{8,9},{9,10},{10,1... | collective-permute-start | bytes 196616 | tf_op jit(solution)/shard_map/while/body/eval_jaxpr/ppermute | solution.py:19
  65.6 4.3 %collective-permute-start = (bf16[4,32,128]{2,1,0:T(8,128)(2,1)S(1)}, bf16[4,32,128]{2,1,0:T(8,128)(2,1)S(1)}, u32[]{:S(2)}, u32[]{:S(2)}) collective-permute-start(bf16[4,32,128]{2,1,0:T(8,128)(2,1)S(1)} %copy.76), channel_id=1, source_target_pairs={{0,1},{1,2},{2,3},{3,0},{4,5},{5,6},{6,7},{7,4},{8,9},{9,10},{10,1... | collective-permute-start | bytes 98312 | tf_op jit(solution)/shard_map/while/body/eval_jaxpr/ppermute | solution.py:19
  66.8 3.0 %collective-permute-start.1 = (f32[4,32]{1,0:T(4,128)S(1)}, f32[4,32]{1,0:T(4,128)S(1)}, u32[]{:S(2)}, u32[]{:S(2)}) collective-permute-start(f32[4,32]{1,0:T(4,128)S(1)} %get-tuple-element.343), channel_id=1, source_target_pairs={{0,1},{1,2},{2,3},{3,0},{4,5},{5,6},{6,7},{7,4},{8,9},{9,10},{10,1... | collective-permute-start | bytes 1544 | tf_op jit(solution)/shard_map/while/body/eval_jaxpr/ppermute | solution.py:19
  66.9 3.0 %collective-permute-start.2 = (f32[4,32]{1,0:T(4,128)S(1)}, f32[4,32]{1,0:T(4,128)S(1)}, u32[]{:S(2)}, u32[]{:S(2)}) collective-permute-start(f32[4,32]{1,0:T(4,128)S(1)} %get-tuple-element.344), channel_id=1, source_target_pairs={{0,1},{1,2},{2,3},{3,0},{4,5},{5,6},{6,7},{7,4},{8,9},{9,10},{10,1... | collective-permute-start | bytes 1544 | tf_op jit(solution)/shard_map/while/body/eval_jaxpr/ppermute | solution.py:19
  71.0 4.2 %collective-permute-start.3 = (f32[4,32,128]{2,1,0:T(8,128)S(1)}, f32[4,32,128]{2,1,0:T(8,128)S(1)}, u32[]{:S(2)}, u32[]{:S(2)}) collective-permute-start(f32[4,32,128]{2,1,0:T(8,128)S(1)} %fusion.37), channel_id=1, source_target_pairs={{0,1},{1,2},{2,3},{3,0},{4,5},{5,6},{6,7},{7,4},{8,9},{9,10},{10,1... | collective-permute-start | bytes 196616 | tf_op jit(solution)/shard_map/while/body/eval_jaxpr/ppermute | solution.py:19
  71.1 4.1 %collective-permute-start = (bf16[4,32,128]{2,1,0:T(8,128)(2,1)S(1)}, bf16[4,32,128]{2,1,0:T(8,128)(2,1)S(1)}, u32[]{:S(2)}, u32[]{:S(2)}) collective-permute-start(bf16[4,32,128]{2,1,0:T(8,128)(2,1)S(1)} %copy.76), channel_id=1, source_target_pairs={{0,1},{1,2},{2,3},{3,0},{4,5},{5,6},{6,7},{7,4},{8,9},{9,10},{10,1... | collective-permute-start | bytes 98312 | tf_op jit(solution)/shard_map/while/body/eval_jaxpr/ppermute | solution.py:19
  72.1 3.0 %collective-permute-start.1 = (f32[4,32]{1,0:T(4,128)S(1)}, f32[4,32]{1,0:T(4,128)S(1)}, u32[]{:S(2)}, u32[]{:S(2)}) collective-permute-start(f32[4,32]{1,0:T(4,128)S(1)} %get-tuple-element.343), channel_id=1, source_target_pairs={{0,1},{1,2},{2,3},{3,0},{4,5},{5,6},{6,7},{7,4},{8,9},{9,10},{10,1... | collective-permute-start | bytes 1544 | tf_op jit(solution)/shard_map/while/body/eval_jaxpr/ppermute | solution.py:19
  72.2 3.0 %collective-permute-start.2 = (f32[4,32]{1,0:T(4,128)S(1)}, f32[4,32]{1,0:T(4,128)S(1)}, u32[]{:S(2)}, u32[]{:S(2)}) collective-permute-start(f32[4,32]{1,0:T(4,128)S(1)} %get-tuple-element.344), channel_id=1, source_target_pairs={{0,1},{1,2},{2,3},{3,0},{4,5},{5,6},{6,7},{7,4},{8,9},{9,10},{10,1... | collective-permute-start | bytes 1544 | tf_op jit(solution)/shard_map/while/body/eval_jaxpr/ppermute | solution.py:19
Sparse Core Ops, SparseCore 0:
  128.4 28.9 reduce-scatter.3
where the time goes:
time: 166 us
  blocking collectives  74.5 us (45%)
  waiting for transfers between devices  37.4 us (23%)
  matrix products  20.5 us (12%)
  between operations  14.1 us (8%)
  starting transfers between devices  9.21 us (6%)
  local copies, waits for them, and re-layouts  7.76 us (5%)
  other arithmetic  2.39 us (1%)
    unnamed x2, waiting for transfers between devices  29.2 us
    unnamed x1, blocking collectives  19.6 us
    unnamed x1, matrix products  18.2 us
    all_gather x1, blocking collectives, per_device(): lax.all_gather(new_keys, 'beam', axis=0, tiled=True)  15 us
    all_gather x1, blocking collectives, per_device(): lax.all_gather(queries, 'beam', axis=0, tiled=True)  13.4 us
    all_gather x1, blocking collectives, per_device(): lax.all_gather(new_values, 'beam', axis=0, tiled=True)  13.4 us
    all_gather x1, blocking collectives, per_device(): all_beams = lax.all_gather(attended, 'beam', axis=0, tiled=True)  13.1 us
    ppermute x16, starting transfers between devices, shifted(): lax.ppermute(array, axis, [(i, (i + by) % length) for i in range(length)])  9.2 us
  transfers between devices with their start and end apart: 17, of which 9 were waited for; matrix products, arithmetic and copies ran while one was open for 0% of the time, Pallas kernels for 0%

commit v1 on v0

v1 whole, which is shorter than its diff:
```python
import math

import jax
import jax.numpy as jnp
from jax import lax
from jax.experimental import pallas as pl
from jax.experimental.pallas import tpu as pltpu
from jax.sharding import PartitionSpec as P

H = 128
KVH = 8
HD = 128
SPAN = 128
GROUP = H // KVH

MASKED = -1e30
SCALE = 1.0 / math.sqrt(HD)

BF = jnp.bfloat16
F32 = jnp.float32
VMEM = pl.BlockSpec(memory_space=pltpu.VMEM)
SMEM = pl.BlockSpec(memory_space=pltpu.SMEM)


def params(mib):
    return pltpu.CompilerParams(vmem_limit_bytes=mib << 20)


def cost(flops, moved):
    return pl.CostEstimate(flops=flops, bytes_accessed=moved, transcendentals=0)


def partner(array, axis, k):
    length = lax.axis_size(axis)
    return lax.ppermute(array, axis, [(i, i ^ k) for i in range(length)])


def pack_kernel(heads, kv_count, q_ref, k_ref, v_ref, out_ref, rows):
    start = lax.axis_index("ctx") * heads // GROUP
    rows[...] = jnp.zeros_like(rows)
    for h in range(heads):
        rows[h : h + 1, :] = q_ref[:, h * HD : (h + 1) * HD].astype(F32)
    for r in range(kv_count):
        here = pl.ds(pl.multiple_of((start + r) * HD, HD), HD)
        rows[heads + r : heads + r + 1, :] = k_ref[:, here].astype(F32)
        rows[heads + kv_count + r : heads + kv_count + r + 1, :] = v_ref[:, here].astype(F32)
    out_ref[...] = rows[...].astype(BF)


def split3(x):
    a = x.astype(BF)
    rest = x - a.astype(F32)
    b = rest.astype(BF)
    c = (rest - b.astype(F32)).astype(BF)
    return a, b, c


def eye(rows):
    shape = (rows, HD)
    return lax.broadcasted_iota(jnp.int32, shape, 0) == lax.broadcasted_iota(jnp.int32, shape, 1)


def attend_kernel(ctx_count, beams, heads, kv_count, per_kv, tokens, *refs):
    lengths, refs = refs[0], refs[1:]
    stacks, (kt, vt), outs = refs[:ctx_count], refs[ctx_count : ctx_count + 2], refs[ctx_count + 2 :]
    c = lax.axis_index("ctx")
    limit = lengths[lax.axis_index("beam")] * SPAN - c * tokens
    rows = beams * per_kv
    keep = lax.broadcasted_iota(jnp.int32, (rows, tokens), 1) < limit
    for k in range(ctx_count):
        first = (c ^ k) * heads // GROUP
        lses = []
        for r in range(kv_count):
            q = stacks[k][:, r * per_kv : (r + 1) * per_kv, :].astype(F32)
            q = q.reshape(rows, HD).astype(BF)
            s = lax.dot_general(q, kt[first + r], (((1,), (1,)), ((), ())), preferred_element_type=F32)
            s = jnp.where(keep, s * SCALE, MASKED)
            peak = jnp.max(s, axis=-1, keepdims=True)
            w = jnp.where(keep, jnp.exp(s - peak), 0.0)
            total = jnp.sum(w, axis=-1, keepdims=True)
            o = jnp.dot(w.astype(BF), vt[first + r], preferred_element_type=F32)
            some = total > 0.0
            safe = jnp.where(some, total, 1.0)
            outs[k][r * rows : (r + 1) * rows, :] = (o / safe).astype(BF)
            lses.append(jnp.where(some, peak + jnp.log(safe), MASKED))
        lse = jnp.concatenate(lses, axis=0) if kv_count > 1 else lses[0]
        count = kv_count * rows
        line = jnp.sum(jnp.where(eye(count), lse, 0.0), axis=0, keepdims=True)
        parts = [p.astype(F32) for p in split3(line)]
        which = lax.broadcasted_iota(jnp.int32, (16, HD), 0)
        stats = jnp.where(which == 0, parts[0], jnp.where(which == 1, parts[1], jnp.where(which == 2, parts[2], 0.0)))
        outs[k][count : count + 16, :] = stats.astype(BF)


def merge_kernel(ctx_count, beams, heads, kv_count, per_kv, *refs):
    stack, states, out_ref = refs[0], refs[1 : 1 + ctx_count], refs[1 + ctx_count]
    b = lax.axis_index("beam")
    rows = beams * per_kv
    count = kv_count * rows
    diagonal = eye(count)
    own, value = [], []
    for r in range(kv_count):
        q = stack[:, r * per_kv : (r + 1) * per_kv, :].astype(F32)
        key = stack[:, heads + r : heads + r + 1, :].astype(F32)
        own.append(jnp.sum(q * key, axis=-1, keepdims=True).reshape(rows, 1) * SCALE)
        v = stack[:, heads + kv_count + r : heads + kv_count + r + 1, :].astype(F32)
        value.append(jnp.broadcast_to(v, (beams, per_kv, HD)).reshape(rows, HD))
    own = jnp.concatenate(own, axis=0) if kv_count > 1 else own[0]
    value = jnp.concatenate(value, axis=0) if kv_count > 1 else value[0]
    lses = []
    for k in range(ctx_count):
        line = states[k][count : count + 16, :].astype(F32)
        line = line[0:1] + line[1:2] + line[2:3]
        lses.append(jnp.sum(jnp.where(diagonal, line, 0.0), axis=-1, keepdims=True))
    peak = own
    for lse in lses:
        peak = jnp.maximum(peak, lse)
    weight = jnp.exp(own - peak)
    total = weight
    blended = weight * value
    for k in range(ctx_count):
        weight = jnp.exp(lses[k] - peak)
        total = total + weight
        blended = blended + weight * states[k][0:count, :].astype(F32)
    result = (blended / total).astype(BF)
    for r in range(kv_count):
        for i in range(beams):
            at = r * rows + i * per_kv
            out_ref[b ^ i, r * per_kv : (r + 1) * per_kv, :] = result[at : at + per_kv, :]


def project_kernel(ctx_count, beams, heads, *refs):
    parents, rows_of, weight = refs[0], refs[1 : 1 + beams], refs[1 + beams]
    outs, (laid, wide) = refs[2 + beams : 2 + beams + ctx_count], refs[2 + beams + ctx_count :]
    b = lax.axis_index("beam")
    c = lax.axis_index("ctx")
    laid[...] = jnp.zeros_like(laid)
    for i in range(beams):
        source = parents[i] ^ b
        row = rows_of[0][i].astype(F32)
        for k in range(1, beams):
            row = jnp.where(source == k, rows_of[k][i].astype(F32), row)
        laid[i * heads : (i + 1) * heads, :] = row
    for h in range(heads):
        wide[:, h * HD : (h + 1) * HD] = laid[pl.ds(h, 8, stride=heads), :].astype(BF)
    columns = weight.shape[1] // ctx_count
    step = min(512, columns)
    for k in range(ctx_count):
        for j in range(columns // step):
            at = pl.multiple_of((c ^ k) * columns + j * step, 128)
            part = jnp.dot(wide[...], weight[:, pl.ds(at, step)], preferred_element_type=F32)
            outs[k][:, j * step : (j + 1) * step] = part[:beams]


def per_device(
    queries, new_keys, new_values, cache_keys, cache_values, parents, lengths, out_weight
):
    ctx_count = lax.axis_size("ctx")
    beams = lax.axis_size("beam")
    heads = queries.shape[1] // HD
    tokens = cache_keys.shape[1]
    kv_count = max(1, heads // GROUP)
    per_kv = min(heads, GROUP)
    packet_rows = -(-(heads + 2 * kv_count) // 16) * 16
    count = beams * heads

    packet = pl.pallas_call(
        lambda *refs: pack_kernel(heads, kv_count, *refs),
        out_shape=jax.ShapeDtypeStruct((packet_rows, HD), BF),
        in_specs=[VMEM] * 3,
        out_specs=VMEM,
        scratch_shapes=[pltpu.VMEM((packet_rows, HD), F32)],
        compiler_params=params(4),
        name="pack",
    )(queries, new_keys, new_values)
    kt = jnp.transpose(cache_keys[0], (1, 0, 2))
    vt = jnp.transpose(cache_values[0], (1, 0, 2))
    stack = jnp.stack([packet] + [partner(packet, "beam", k) for k in range(1, beams)])
    stacks = [stack] + [partner(stack, "ctx", k) for k in range(1, ctx_count)]

    state = jax.ShapeDtypeStruct((count + 16, HD), BF)
    states = pl.pallas_call(
        lambda *refs: attend_kernel(ctx_count, beams, heads, kv_count, per_kv, tokens, *refs),
        out_shape=[state] * ctx_count,
        in_specs=[SMEM] + [VMEM] * (ctx_count + 2),
        out_specs=[VMEM] * ctx_count,
        compiler_params=params(8),
        cost_estimate=cost(4 * beams * H * tokens * HD, 4 * tokens * KVH * HD),
        name="attend",
    )(lengths, *stacks, kt, vt)
    states = [states[0]] + [partner(states[k], "ctx", k) for k in range(1, ctx_count)]

    attended = pl.pallas_call(
        lambda *refs: merge_kernel(ctx_count, beams, heads, kv_count, per_kv, *refs),
        out_shape=jax.ShapeDtypeStruct((beams, heads, HD), BF),
        in_specs=[VMEM] * (1 + ctx_count),
        out_specs=VMEM,
        compiler_params=params(8),
        name="merge",
    )(stack, *states)
    rows_of = [attended] + [partner(attended, "beam", k) for k in range(1, beams)]

    columns = out_weight.shape[1] // ctx_count
    parts = pl.pallas_call(
        lambda *refs: project_kernel(ctx_count, beams, heads, *refs),
        out_shape=[jax.ShapeDtypeStruct((beams, columns), F32)] * ctx_count,
        in_specs=[SMEM] + [VMEM] * (beams + 1),
        out_specs=[VMEM] * ctx_count,
        scratch_shapes=[pltpu.VMEM((8 * heads, HD), F32), pltpu.VMEM((8, heads * HD), BF)],
        compiler_params=params(8),
        cost_estimate=cost(16 * out_weight.size, 2 * out_weight.size),
        name="project",
    )(parents, *rows_of, out_weight)
    total = parts[0]
    for k in range(1, ctx_count):
        total = total + partner(parts[k], "ctx", k)
    return total.astype(BF)


def solution(mesh):
    placed = (
        P(("groups", "beam"), "ctx"),
        P(("groups", "beam"), None),
        P(("groups", "beam"), None),
        P(("groups", "beam"), "ctx", None, None),
        P(("groups", "beam"), "ctx", None, None),
        P("groups"),
        P("groups"),
        P("ctx", "beam"),
    )
    return jax.shard_map(
        per_device,
        mesh=mesh,
        in_specs=placed,
        out_specs=P("groups", ("beam", "ctx")),
        check_vma=False,
    )
```

time: 166 us -> 53.7 us (0.32)
  blocking collectives: 74.5 us -> 0 us
  waiting for transfers between devices: 37.4 us -> 12.6 us
  matrix products: 20.5 us -> 0 us
  between operations: 14.1 us -> 0.05 us
  Pallas kernels: 0 us -> 8.24 us
  local copies, waits for them, and re-layouts: 7.76 us -> 15.9 us
  starting transfers between devices: 9.21 us -> 16 us
  other arithmetic: 2.39 us -> 0.62 us
    all_gather x4 -> x0, blocking collectives: 54.9 us -> none  [the longest x1 15 us: per_device(): lax.all_gather(new_keys, 'beam', axis=0, tiled=True)]
    unnamed x2 -> x0, waiting for transfers between devices: 29.2 us -> none
    unnamed x1 -> x0, blocking collectives: 19.6 us -> none
    unnamed x1 -> x0, matrix products: 18.2 us -> none
    unnamed x6 -> x12, local copies, waits for them, and re-layouts: 3.76 us -> 13.9 us
    pallas_call x0 -> x4, Pallas kernels: none -> 8.24 us  [the longest x1 5.03 us: per_device(): pl.pallas_call(lambda *refs: project_kernel(ctx_count, beams, heads, *ref...]
    ppermute x16 -> x15, starting transfers between devices: 9.2 us -> 16 us  [partner(): return lax.ppermute(array, axis, [(i, i ^ k) for i in range(length)])]
    ppermute x16 -> x15, waiting for transfers between devices: 8.24 us -> 12.6 us  [partner(): return lax.ppermute(array, axis, [(i, i ^ k) for i in range(length)])]
  transfers between devices with their start and end apart: 17 -> 15, of which waited for: 9 -> 11; matrix products, arithmetic and copies ran while one was open for 0% -> 4% of each run, Pallas kernels for 0% -> 0%
where the time goes in v1:
time: 53.7 us; the launch traced here: 53.4 us
  starting transfers between devices  16 us (30%)
  local copies, waits for them, and re-layouts  15.9 us (30%)
  waiting for transfers between devices  12.6 us (23%)
  Pallas kernels  8.24 us (15%)
  other arithmetic  0.62 us (1%)
    ppermute x15, starting transfers between devices, partner(): return lax.ppermute(array, axis, [(i, i ^ k) for i in range(length)])  16 us
    unnamed x12, local copies, waits for them, and re-layouts  13.9 us
    ppermute x15, waiting for transfers between devices, partner(): return lax.ppermute(array, axis, [(i, i ^ k) for i in range(length)])  12.6 us
    pallas_call x1, Pallas kernels, per_device(): pl.pallas_call(lambda *refs: project_kernel(ctx_count, beams, heads, *ref...  5.03 us
    pallas_call x1, Pallas kernels, per_device(): pl.pallas_call(lambda *refs: attend_kernel(ctx_count, beams, heads, kv_co...  2.79 us
    transpose x1, local copies, waits for them, and re-layouts, per_device(): vt = jnp.transpose(cache_values[0], (1, 0, 2))  1.92 us
  transfers between devices with their start and end apart: 15, of which 11 were waited for; matrix products, arithmetic and copies ran while one was open for 4% of the time, Pallas kernels for 0%

profile of v1, /device:TPU:0, one launch (start us, length us, event | category | flops | bytes accessed | tf_op | source)
XLA Modules:
  0.0 53.4 jit_solution(4147156738435949587)
XLA Ops:
  0.0 0.7 %copy-done.1 = bf16[1,4096]{1,0:T(2,128)(2,1)S(1)} copy-done((bf16[1,4096]{1,0:T(2,128)(2,1)S(1)}, bf16[1,4096]{1,0:T(2,128)(2,1)}, u32[]{:S(2)}) %copy-start.1) | copy-done | bytes 8216
  0.7 0.7 %copy-done.2 = bf16[1,1024]{1,0:T(2,128)(2,1)S(1)} copy-done((bf16[1,1024]{1,0:T(2,128)(2,1)S(1)}, bf16[1,1024]{1,0:T(2,128)(2,1)}, u32[]{:S(2)}) %copy-start.2) | copy-done | bytes 2072
  1.4 0.7 %copy-done.3 = bf16[1,1024]{1,0:T(2,128)(2,1)S(1)} copy-done((bf16[1,1024]{1,0:T(2,128)(2,1)S(1)}, bf16[1,1024]{1,0:T(2,128)(2,1)}, u32[]{:S(2)}) %copy-start.3) | copy-done | bytes 2072
  2.1 5.1 %collective-permute-start.2 = (bf16[48,128]{1,0:T(8,128)(2,1)S(1)}, bf16[48,128]{1,0:T(8,128)(2,1)S(1)}, u32[]{:S(2)}, u32[]{:S(2)}) collective-permute-start(bf16[48,128]{1,0:T(8,128)(2,1)S(1)} %pack.1), channel_id=1, source_target_pairs={{0,12},{4,8},{8,4},{12,0},{1,13},{5,9},{9,5},{13,1},{2,14},{6,10},... | collective-permute-start | bytes 36872 | tf_op jit(solution)/shard_map/ppermute | solution.py:35
  7.3 0.6 %collective-permute-start = (bf16[48,128]{1,0:T(8,128)(2,1)S(1)}, bf16[48,128]{1,0:T(8,128)(2,1)S(1)}, u32[]{:S(2)}, u32[]{:S(2)}) collective-permute-start(bf16[48,128]{1,0:T(8,128)(2,1)S(1)} %pack.1), channel_id=1, source_target_pairs={{0,4},{4,0},{8,12},{12,8},{1,5},{5,1},{9,13},{13,9},{2,6},{6,2},{1... | collective-permute-start | bytes 36872 | tf_op jit(solution)/shard_map/ppermute | solution.py:35
  7.9 1.0 %collective-permute-done.2 = bf16[48,128]{1,0:T(8,128)(2,1)S(1)} collective-permute-done((bf16[48,128]{1,0:T(8,128)(2,1)S(1)}, bf16[48,128]{1,0:T(8,128)(2,1)S(1)}, u32[]{:S(2)}, u32[]{:S(2)}) %collective-permute-start.2) | collective-permute-done | bytes 12320 | tf_op jit(solution)/shard_map/ppermute | solution.py:35
  8.9 2.9 %collective-permute-done.1 = bf16[48,128]{1,0:T(8,128)(2,1)S(1)} collective-permute-done((bf16[48,128]{1,0:T(8,128)(2,1)S(1)}, bf16[48,128]{1,0:T(8,128)(2,1)S(1)}, u32[]{:S(2)}, u32[]{:S(2)}) %collective-permute-start.1) | collective-permute-done | bytes 12320 | tf_op jit(solution)/shard_map/ppermute | solution.py:35
  12.0 1.6 %collective-permute-start.4 = (bf16[4,48,128]{2,1,0:T(8,128)(2,1)S(1)}, bf16[4,48,128]{2,1,0:T(8,128)(2,1)S(1)}, u32[]{:S(2)}, u32[]{:S(2)}) collective-permute-start(bf16[4,48,128]{2,1,0:T(8,128)(2,1)S(1)} %pad_maximum_fusion.refs_1_.refs_0_), channel_id=1, source_target_pairs={{0,2},{1,3},{2,0},{3,1},{4,6},{5,7},{6,4},{7,5},{8,10},{9,11},{10,... | collective-permute-start | bytes 147464 | tf_op jit(solution)/shard_map/ppermute | solution.py:35
  13.5 0.3 collective-permute-start.3
  13.8 1.9 %copy_bitcast_fusion = (bf16[8,512,128]{2,1,0:T(8,128)(2,1)S(1)}, bf16[8,512,128]{2,1,0:T(8,128)(2,1)S(1)}) fusion(bf16[1,512,8,128]{3,2,1,0:T(8,128)(2,1)} %param.12, bf16[1,512,8,128]{3,2,1,0:T(8,128)(2,1)} %param.11), kind=kLoop, calls=%fused_computation | loop fusion | bytes 4194304 | tf_op jit(solution)/shard_map/transpose | solution.py:177
  15.9 0.9 %collective-permute-done.4.refs_3_ = bf16[4,48,128]{2,1,0:T(8,128)(2,1)S(1)} collective-permute-done((bf16[4,48,128]{2,1,0:T(8,128)(2,1)S(1)}, bf16[4,48,128]{2,1,0:T(8,128)(2,1)S(1)}, u32[]{:S(2)}, u32[]{:S(2)}) %collective-permute-start.4) | collective-permute-done | bytes 49184 | tf_op jit(solution)/shard_map/ppermute | solution.py:35
  16.9 0.7 %copy-done.4 = s32[4]{0:T(128)S(1)} copy-done((s32[4]{0:T(128)S(1)}, s32[4]{0:T(128)}, u32[]{:S(2)}) %copy-start.4) | copy-done | bytes 40
  17.5 2.8 %attend.1 = (bf16[144,128]{1,0:T(8,128)(2,1)S(1)}, bf16[144,128]{1,0:T(8,128)(2,1)S(1)}, bf16[144,128]{1,0:T(8,128)(2,1)S(1)}, bf16[144,128]{1,0:T(8,128)(2,1)S(1)}) custom-call(s32[4]{0:T(128)S(1)} %copy-done.4, bf16[4,48,128]{2,1,0:T(8,128)(2,1)S(1)} %pad_maximum_fusion.refs_1_.refs_0_, bf16[4,48,128]{2,1,0:T(8,128)(2,1)S(1)} %collective-permute-done.3.refs_2_, ...), custom_call_target="tpu_custom_call" | custom-call | flops 134217728 | bytes 2097152 | tf_op jit(solution)/shard_map/attend/pallas_call | solution.py:182
  20.5 1.1 %collective-permute-start.7 = (bf16[144,128]{1,0:T(8,128)(2,1)S(1)}, bf16[144,128]{1,0:T(8,128)(2,1)S(1)}, u32[]{:S(2)}, u32[]{:S(2)}) collective-permute-start(bf16[144,128]{1,0:T(8,128)(2,1)S(1)} %get-tuple-element.15), channel_id=1, source_target_pairs={{0,2},{1,3},{2,0},{3,1},{4,6},{5,7},{6,4},{7,5},{8,10},{9,11},{10,... | collective-permute-start | bytes 110600 | tf_op jit(solution)/shard_map/ppermute | solution.py:35
  21.6 0.6 %collective-permute-start.8 = (bf16[144,128]{1,0:T(8,128)(2,1)S(1)}, bf16[144,128]{1,0:T(8,128)(2,1)S(1)}, u32[]{:S(2)}, u32[]{:S(2)}) collective-permute-start(bf16[144,128]{1,0:T(8,128)(2,1)S(1)} %get-tuple-element.16), channel_id=1, source_target_pairs={{0,3},{1,2},{2,1},{3,0},{4,7},{5,6},{6,5},{7,4},{8,11},{9,10},{10,... | collective-permute-start | bytes 110600 | tf_op jit(solution)/shard_map/ppermute | solution.py:35
  22.2 2.2 %collective-permute-done.7.refs_3_ = bf16[144,128]{1,0:T(8,128)(2,1)S(1)} collective-permute-done((bf16[144,128]{1,0:T(8,128)(2,1)S(1)}, bf16[144,128]{1,0:T(8,128)(2,1)S(1)}, u32[]{:S(2)}, u32[]{:S(2)}) %collective-permute-start.7) | collective-permute-done | bytes 36896 | tf_op jit(solution)/shard_map/ppermute | solution.py:35
  24.4 0.6 %collective-permute-done.8.refs_4_ = bf16[144,128]{1,0:T(8,128)(2,1)S(1)} collective-permute-done((bf16[144,128]{1,0:T(8,128)(2,1)S(1)}, bf16[144,128]{1,0:T(8,128)(2,1)S(1)}, u32[]{:S(2)}, u32[]{:S(2)}) %collective-permute-start.8) | collective-permute-done | bytes 36896 | tf_op jit(solution)/shard_map/ppermute | solution.py:35
  25.1 0.4 merge.1.refs_1_
  25.5 1.5 %collective-permute-start.11 = (bf16[4,32,128]{2,1,0:T(8,128)(2,1)S(1)}, bf16[4,32,128]{2,1,0:T(8,128)(2,1)S(1)}, u32[]{:S(2)}, u32[]{:S(2)}) collective-permute-start(bf16[4,32,128]{2,1,0:T(8,128)(2,1)S(1)} %merge.1.refs_1_), channel_id=1, source_target_pairs={{0,12},{4,8},{8,4},{12,0},{1,13},{5,9},{9,5},{13,1},{2,14},{6,10},... | collective-permute-start | bytes 98312 | tf_op jit(solution)/shard_map/ppermute | solution.py:35
  27.0 0.6 %collective-permute-start.10 = (bf16[4,32,128]{2,1,0:T(8,128)(2,1)S(1)}, bf16[4,32,128]{2,1,0:T(8,128)(2,1)S(1)}, u32[]{:S(2)}, u32[]{:S(2)}) collective-permute-start(bf16[4,32,128]{2,1,0:T(8,128)(2,1)S(1)} %merge.1.refs_1_), channel_id=1, source_target_pairs={{0,8},{4,12},{8,0},{12,4},{1,9},{5,13},{9,1},{13,5},{2,10},{6,14},... | collective-permute-start | bytes 98312 | tf_op jit(solution)/shard_map/ppermute | solution.py:35
  27.6 2.3 %collective-permute-start.9 = (bf16[4,32,128]{2,1,0:T(8,128)(2,1)S(1)}, bf16[4,32,128]{2,1,0:T(8,128)(2,1)S(1)}, u32[]{:S(2)}, u32[]{:S(2)}) collective-permute-start(bf16[4,32,128]{2,1,0:T(8,128)(2,1)S(1)} %merge.1.refs_1_), channel_id=1, source_target_pairs={{0,4},{4,0},{8,12},{12,8},{1,5},{5,1},{9,13},{13,9},{2,6},{6,2},{1... | collective-permute-start | bytes 98312 | tf_op jit(solution)/shard_map/ppermute | solution.py:35
  29.9 1.6 %collective-permute-done.11.refs_4_ = bf16[4,32,128]{2,1,0:T(8,128)(2,1)S(1)} collective-permute-done((bf16[4,32,128]{2,1,0:T(8,128)(2,1)S(1)}, bf16[4,32,128]{2,1,0:T(8,128)(2,1)S(1)}, u32[]{:S(2)}, u32[]{:S(2)}) %collective-permute-start.11) | collective-permute-done | bytes 32800 | tf_op jit(solution)/shard_map/ppermute | solution.py:35
  31.6 0.4 collective-permute-done.10.refs_3_
  31.9 0.3 collective-permute-done.9.refs_2_
  32.2 10.5 %copy-done = bf16[4096,4096]{1,0:T(8,128)(2,1)S(1)} copy-done((bf16[4096,4096]{1,0:T(8,128)(2,1)S(1)}, bf16[4096,4096]{1,0:T(8,128)(2,1)}, u32[]{:S(2)}) %copy-start) | copy-done | bytes 33554456
  42.8 0.7 %copy-done.5 = s32[4]{0:T(128)S(1)} copy-done((s32[4]{0:T(128)S(1)}, s32[4]{0:T(128)}, u32[]{:S(2)}) %copy-start.5) | copy-done | bytes 40
  43.4 5.0 %project.1 = (f32[4,1024]{1,0:T(4,128)S(1)}, f32[4,1024]{1,0:T(4,128)S(1)}, f32[4,1024]{1,0:T(4,128)S(1)}, f32[4,1024]{1,0:T(4,128)S(1)}) custom-call(s32[4]{0:T(128)S(1)} %copy-done.5, bf16[4,32,128]{2,1,0:T(8,128)(2,1)S(1)} %merge.1.refs_1_, bf16[4,32,128]{2,1,0:T(8,128)(2,1)S(1)} %collective-permute-done.9.refs_2_, ...), custom_call_target="tpu_custom_call" | custom-call | flops 268435456 | bytes 33554432 | tf_op jit(solution)/shard_map/project/pallas_call | solution.py:204
  48.4 1.2 %collective-permute-start.13 = (f32[4,1024]{1,0:T(4,128)S(1)}, f32[4,1024]{1,0:T(4,128)S(1)}, u32[]{:S(2)}, u32[]{:S(2)}) collective-permute-start(f32[4,1024]{1,0:T(4,128)S(1)} %get-tuple-element.19), channel_id=1, source_target_pairs={{0,2},{1,3},{2,0},{3,1},{4,6},{5,7},{6,4},{7,5},{8,10},{9,11},{10,... | collective-permute-start | bytes 49160 | tf_op jit(solution)/shard_map/ppermute | solution.py:35
  49.6 0.7 %collective-permute-start.14 = (f32[4,1024]{1,0:T(4,128)S(1)}, f32[4,1024]{1,0:T(4,128)S(1)}, u32[]{:S(2)}, u32[]{:S(2)}) collective-permute-start(f32[4,1024]{1,0:T(4,128)S(1)} %get-tuple-element.20), channel_id=1, source_target_pairs={{0,3},{1,2},{2,1},{3,0},{4,7},{5,6},{6,5},{7,4},{8,11},{9,10},{10,... | collective-permute-start | bytes 49160 | tf_op jit(solution)/shard_map/ppermute | solution.py:35
  50.3 1.9 %collective-permute-done.13 = f32[4,1024]{1,0:T(4,128)S(1)} collective-permute-done((f32[4,1024]{1,0:T(4,128)S(1)}, f32[4,1024]{1,0:T(4,128)S(1)}, u32[]{:S(2)}, u32[]{:S(2)}) %collective-permute-start.13) | collective-permute-done | bytes 16416 | tf_op jit(solution)/shard_map/ppermute | solution.py:35
  52.2 0.5 %collective-permute-done.14 = f32[4,1024]{1,0:T(4,128)S(1)} collective-permute-done((f32[4,1024]{1,0:T(4,128)S(1)}, f32[4,1024]{1,0:T(4,128)S(1)}, u32[]{:S(2)}, u32[]{:S(2)}) %collective-permute-start.14) | collective-permute-done | bytes 16416 | tf_op jit(solution)/shard_map/ppermute | solution.py:35
  52.8 0.6 %add_convert_fusion = bf16[4,1024]{1,0:T(4,128)(2,1)} fusion(f32[4,1024]{1,0:T(4,128)S(1)} %collective-permute-done.14, f32[4,1024]{1,0:T(4,128)S(1)} %collective-permute-done.13, f32[4,1024]{1,0:T(4,128)S(1)} %get-tuple-element.17, f32[4,1024]{1,0:T(4,128)S(1)} %collective-permute-done.12), kind=kLoop, calls=%fused_computation.3 | loop fusion | flops 16384 | bytes 73728 | tf_op jit(solution)/shard_map/convert_element_type | solution.py:217
  (17 shorter events, 0.5 us)
Async XLA Ops:
  0.0 0.7 %copy-start.1 = (bf16[1,4096]{1,0:T(2,128)(2,1)S(1)}, bf16[1,4096]{1,0:T(2,128)(2,1)}, u32[]{:S(2)}) copy-start(bf16[1,4096]{1,0:T(2,128)(2,1)} %refs_0_.3) | copy-start | bytes 24580
  0.7 0.7 %copy-start.2 = (bf16[1,1024]{1,0:T(2,128)(2,1)S(1)}, bf16[1,1024]{1,0:T(2,128)(2,1)}, u32[]{:S(2)}) copy-start(bf16[1,1024]{1,0:T(2,128)(2,1)} %refs_1_.1) | copy-start | bytes 6148
  1.4 0.7 %copy-start.3 = (bf16[1,1024]{1,0:T(2,128)(2,1)S(1)}, bf16[1,1024]{1,0:T(2,128)(2,1)}, u32[]{:S(2)}) copy-start(bf16[1,1024]{1,0:T(2,128)(2,1)} %refs_2_.1) | copy-start | bytes 6148
  2.1 6.8 %collective-permute-start.2 = (bf16[48,128]{1,0:T(8,128)(2,1)S(1)}, bf16[48,128]{1,0:T(8,128)(2,1)S(1)}, u32[]{:S(2)}, u32[]{:S(2)}) collective-permute-start(bf16[48,128]{1,0:T(8,128)(2,1)S(1)} %pack.1), channel_id=1, source_target_pairs={{0,12},{4,8},{8,4},{12,0},{1,13},{5,9},{9,5},{13,1},{2,14},{6,10},... | collective-permute-start | bytes 36872 | tf_op jit(solution)/shard_map/ppermute | solution.py:35
  7.3 4.6 %collective-permute-start.1 = (bf16[48,128]{1,0:T(8,128)(2,1)S(1)}, bf16[48,128]{1,0:T(8,128)(2,1)S(1)}, u32[]{:S(2)}, u32[]{:S(2)}) collective-permute-start(bf16[48,128]{1,0:T(8,128)(2,1)S(1)} %pack.1), channel_id=1, source_target_pairs={{0,8},{4,12},{8,0},{12,4},{1,9},{5,13},{9,1},{13,5},{2,10},{6,14},... | collective-permute-start | bytes 36872 | tf_op jit(solution)/shard_map/ppermute | solution.py:35
  7.3 4.6 %collective-permute-start = (bf16[48,128]{1,0:T(8,128)(2,1)S(1)}, bf16[48,128]{1,0:T(8,128)(2,1)S(1)}, u32[]{:S(2)}, u32[]{:S(2)}) collective-permute-start(bf16[48,128]{1,0:T(8,128)(2,1)S(1)} %pack.1), channel_id=1, source_target_pairs={{0,4},{4,0},{8,12},{12,8},{1,5},{5,1},{9,13},{13,9},{2,6},{6,2},{1... | collective-permute-start | bytes 36872 | tf_op jit(solution)/shard_map/ppermute | solution.py:35
  11.9 4.0 %collective-permute-start.5 = (bf16[4,48,128]{2,1,0:T(8,128)(2,1)S(1)}, bf16[4,48,128]{2,1,0:T(8,128)(2,1)S(1)}, u32[]{:S(2)}, u32[]{:S(2)}) collective-permute-start(bf16[4,48,128]{2,1,0:T(8,128)(2,1)S(1)} %pad_maximum_fusion.refs_1_.refs_0_), channel_id=1, source_target_pairs={{0,3},{1,2},{2,1},{3,0},{4,7},{5,6},{6,5},{7,4},{8,11},{9,10},{10,... | collective-permute-start | bytes 147464 | tf_op jit(solution)/shard_map/ppermute | solution.py:35
  12.0 4.9 %collective-permute-start.4 = (bf16[4,48,128]{2,1,0:T(8,128)(2,1)S(1)}, bf16[4,48,128]{2,1,0:T(8,128)(2,1)S(1)}, u32[]{:S(2)}, u32[]{:S(2)}) collective-permute-start(bf16[4,48,128]{2,1,0:T(8,128)(2,1)S(1)} %pad_maximum_fusion.refs_1_.refs_0_), channel_id=1, source_target_pairs={{0,2},{1,3},{2,0},{3,1},{4,6},{5,7},{6,4},{7,5},{8,10},{9,11},{10,... | collective-permute-start | bytes 147464 | tf_op jit(solution)/shard_map/ppermute | solution.py:35
  13.5 3.3 %collective-permute-start.3 = (bf16[4,48,128]{2,1,0:T(8,128)(2,1)S(1)}, bf16[4,48,128]{2,1,0:T(8,128)(2,1)S(1)}, u32[]{:S(2)}, u32[]{:S(2)}) collective-permute-start(bf16[4,48,128]{2,1,0:T(8,128)(2,1)S(1)} %pad_maximum_fusion.refs_1_.refs_0_), channel_id=1, source_target_pairs={{0,1},{1,0},{2,3},{3,2},{4,5},{5,4},{6,7},{7,6},{8,9},{9,8},{10,11... | collective-permute-start | bytes 147464 | tf_op jit(solution)/shard_map/ppermute | solution.py:35
  16.8 0.7 %copy-start.4 = (s32[4]{0:T(128)S(1)}, s32[4]{0:T(128)}, u32[]{:S(2)}) copy-start(s32[4]{0:T(128)} %refs_0_.4) | copy-start | bytes 52
  20.3 1.9 %collective-permute-start.6 = (bf16[144,128]{1,0:T(8,128)(2,1)S(1)}, bf16[144,128]{1,0:T(8,128)(2,1)S(1)}, u32[]{:S(2)}, u32[]{:S(2)}) collective-permute-start(bf16[144,128]{1,0:T(8,128)(2,1)S(1)} %get-tuple-element.14), channel_id=1, source_target_pairs={{0,1},{1,0},{2,3},{3,2},{4,5},{5,4},{6,7},{7,6},{8,9},{9,8},{10,11... | collective-permute-start | bytes 110600 | tf_op jit(solution)/shard_map/ppermute | solution.py:35
  20.5 4.0 %collective-permute-start.7 = (bf16[144,128]{1,0:T(8,128)(2,1)S(1)}, bf16[144,128]{1,0:T(8,128)(2,1)S(1)}, u32[]{:S(2)}, u32[]{:S(2)}) collective-permute-start(bf16[144,128]{1,0:T(8,128)(2,1)S(1)} %get-tuple-element.15), channel_id=1, source_target_pairs={{0,2},{1,3},{2,0},{3,1},{4,6},{5,7},{6,4},{7,5},{8,10},{9,11},{10,... | collective-permute-start | bytes 110600 | tf_op jit(solution)/shard_map/ppermute | solution.py:35
  21.6 3.4 %collective-permute-start.8 = (bf16[144,128]{1,0:T(8,128)(2,1)S(1)}, bf16[144,128]{1,0:T(8,128)(2,1)S(1)}, u32[]{:S(2)}, u32[]{:S(2)}) collective-permute-start(bf16[144,128]{1,0:T(8,128)(2,1)S(1)} %get-tuple-element.16), channel_id=1, source_target_pairs={{0,3},{1,2},{2,1},{3,0},{4,7},{5,6},{6,5},{7,4},{8,11},{9,10},{10,... | collective-permute-start | bytes 110600 | tf_op jit(solution)/shard_map/ppermute | solution.py:35
  25.5 6.1 %collective-permute-start.11 = (bf16[4,32,128]{2,1,0:T(8,128)(2,1)S(1)}, bf16[4,32,128]{2,1,0:T(8,128)(2,1)S(1)}, u32[]{:S(2)}, u32[]{:S(2)}) collective-permute-start(bf16[4,32,128]{2,1,0:T(8,128)(2,1)S(1)} %merge.1.refs_1_), channel_id=1, source_target_pairs={{0,12},{4,8},{8,4},{12,0},{1,13},{5,9},{9,5},{13,1},{2,14},{6,10},... | collective-permute-start | bytes 98312 | tf_op jit(solution)/shard_map/ppermute | solution.py:35
  27.0 5.0 %collective-permute-start.10 = (bf16[4,32,128]{2,1,0:T(8,128)(2,1)S(1)}, bf16[4,32,128]{2,1,0:T(8,128)(2,1)S(1)}, u32[]{:S(2)}, u32[]{:S(2)}) collective-permute-start(bf16[4,32,128]{2,1,0:T(8,128)(2,1)S(1)} %merge.1.refs_1_), channel_id=1, source_target_pairs={{0,8},{4,12},{8,0},{12,4},{1,9},{5,13},{9,1},{13,5},{2,10},{6,14},... | collective-permute-start | bytes 98312 | tf_op jit(solution)/shard_map/ppermute | solution.py:35
  27.6 4.6 %collective-permute-start.9 = (bf16[4,32,128]{2,1,0:T(8,128)(2,1)S(1)}, bf16[4,32,128]{2,1,0:T(8,128)(2,1)S(1)}, u32[]{:S(2)}, u32[]{:S(2)}) collective-permute-start(bf16[4,32,128]{2,1,0:T(8,128)(2,1)S(1)} %merge.1.refs_1_), channel_id=1, source_target_pairs={{0,4},{4,0},{8,12},{12,8},{1,5},{5,1},{9,13},{13,9},{2,6},{6,2},{1... | collective-permute-start | bytes 98312 | tf_op jit(solution)/shard_map/ppermute | solution.py:35
  32.2 10.5 %copy-start = (bf16[4096,4096]{1,0:T(8,128)(2,1)S(1)}, bf16[4096,4096]{1,0:T(8,128)(2,1)}, u32[]{:S(2)}) copy-start(bf16[4096,4096]{1,0:T(8,128)(2,1)} %refs_5_.1) | copy-start | bytes 100663296
  42.8 0.7 %copy-start.5 = (s32[4]{0:T(128)S(1)}, s32[4]{0:T(128)}, u32[]{:S(2)}) copy-start(s32[4]{0:T(128)} %refs_0_.5) | copy-start | bytes 52
  48.4 1.9 %collective-permute-start.12 = (f32[4,1024]{1,0:T(4,128)S(1)}, f32[4,1024]{1,0:T(4,128)S(1)}, u32[]{:S(2)}, u32[]{:S(2)}) collective-permute-start(f32[4,1024]{1,0:T(4,128)S(1)} %get-tuple-element.18), channel_id=1, source_target_pairs={{0,1},{1,0},{2,3},{3,2},{4,5},{5,4},{6,7},{7,6},{8,9},{9,8},{10,11... | collective-permute-start | bytes 49160 | tf_op jit(solution)/shard_map/ppermute | solution.py:35
  48.4 3.8 %collective-permute-start.13 = (f32[4,1024]{1,0:T(4,128)S(1)}, f32[4,1024]{1,0:T(4,128)S(1)}, u32[]{:S(2)}, u32[]{:S(2)}) collective-permute-start(f32[4,1024]{1,0:T(4,128)S(1)} %get-tuple-element.19), channel_id=1, source_target_pairs={{0,2},{1,3},{2,0},{3,1},{4,6},{5,7},{6,4},{7,5},{8,10},{9,11},{10,... | collective-permute-start | bytes 49160 | tf_op jit(solution)/shard_map/ppermute | solution.py:35
  49.6 3.2 %collective-permute-start.14 = (f32[4,1024]{1,0:T(4,128)S(1)}, f32[4,1024]{1,0:T(4,128)S(1)}, u32[]{:S(2)}, u32[]{:S(2)}) collective-permute-start(f32[4,1024]{1,0:T(4,128)S(1)} %get-tuple-element.20), channel_id=1, source_target_pairs={{0,3},{1,2},{2,1},{3,0},{4,7},{5,6},{6,5},{7,4},{8,11},{9,10},{10,... | collective-permute-start | bytes 49160 | tf_op jit(solution)/shard_map/ppermute | solution.py:35

commit v2 on v1

--- a/solution.py
+++ b/solution.py
@@ -7,6 +7,7 @@
 from jax.experimental.pallas import tpu as pltpu
 from jax.sharding import PartitionSpec as P
 
+
 H = 128
 KVH = 8
 HD = 128
@@ -19,7 +20,8 @@
 BF = jnp.bfloat16
 F32 = jnp.float32
 VMEM = pl.BlockSpec(memory_space=pltpu.VMEM)
-SMEM = pl.BlockSpec(memory_space=pltpu.SMEM)
+HBM = pl.BlockSpec(memory_space=pltpu.HBM)
+PIECES = 4
 
 
 def params(mib):
@@ -30,14 +32,26 @@
     return pl.CostEstimate(flops=flops, bytes_accessed=moved, transcendentals=0)
 
 
-def partner(array, axis, k):
+def partners(arrays, axis):
     length = lax.axis_size(axis)
-    return lax.ppermute(array, axis, [(i, i ^ k) for i in range(length)])
-
-
-def pack_kernel(heads, kv_count, q_ref, k_ref, v_ref, out_ref, rows):
+    found = []
+    for k in range(1, length):
+        array = arrays[k] if isinstance(arrays, (list, tuple)) else arrays
+        found.append(lax.ppermute(array, axis, [(i, i ^ k) for i in range(length)]))
+    return found
+
+
+def pack_kernel(heads, kv_count, q_hbm, k_hbm, v_hbm, out_ref, q_ref, k_ref, v_ref, rows, sems):
+    copies = [
+        pltpu.make_async_copy(src, dst, sems.at[n])
+        for n, (src, dst) in enumerate(((q_hbm, q_ref), (k_hbm, k_ref), (v_hbm, v_ref)))
+    ]
+    for copy in copies:
+        copy.start()
     start = lax.axis_index("ctx") * heads // GROUP
     rows[...] = jnp.zeros_like(rows)
+    for copy in copies:
+        copy.wait()
     for h in range(heads):
         rows[h : h + 1, :] = q_ref[:, h * HD : (h + 1) * HD].astype(F32)
     for r in range(kv_count):
@@ -47,6 +61,13 @@
     out_ref[...] = rows[...].astype(BF)
 
 
+def fetch_kernel(piece, w_hbm, out_ref, sem):
+    rows = out_ref.shape[0]
+    copy = pltpu.make_async_copy(w_hbm.at[pl.ds(piece * rows, rows)], out_ref, sem)
+    copy.start()
+    copy.wait()
+
+
 def split3(x):
     a = x.astype(BF)
     rest = x - a.astype(F32)
@@ -61,10 +82,22 @@
 
 
 def attend_kernel(ctx_count, beams, heads, kv_count, per_kv, tokens, *refs):
-    lengths, refs = refs[0], refs[1:]
-    stacks, (kt, vt), outs = refs[:ctx_count], refs[ctx_count : ctx_count + 2], refs[ctx_count + 2 :]
+    lengths_hbm, parents_hbm, w_hbm, kt, vt = refs[:5]
+    stacks, outs = refs[5 : 5 + ctx_count], refs[5 + ctx_count : 5 + 2 * ctx_count]
+    piece, lengths, parents, sems = refs[5 + 2 * ctx_count :]
+    small = [
+        pltpu.make_async_copy(lengths_hbm, lengths, sems.at[0]),
+        pltpu.make_async_copy(parents_hbm, parents, sems.at[1]),
+    ]
+    large = pltpu.make_async_copy(w_hbm.at[pl.ds(piece.shape[0], piece.shape[0])], piece, sems.at[2])
+    for copy in small:
+        copy.start()
+    large.start()
+    b = lax.axis_index("beam")
     c = lax.axis_index("ctx")
-    limit = lengths[lax.axis_index("beam")] * SPAN - c * tokens
+    for copy in small:
+        copy.wait()
+    limit = lengths[b] * SPAN - c * tokens
     rows = beams * per_kv
     keep = lax.broadcasted_iota(jnp.int32, (rows, tokens), 1) < limit
     for k in range(ctx_count):
@@ -89,7 +122,12 @@
         parts = [p.astype(F32) for p in split3(line)]
         which = lax.broadcasted_iota(jnp.int32, (16, HD), 0)
         stats = jnp.where(which == 0, parts[0], jnp.where(which == 1, parts[1], jnp.where(which == 2, parts[2], 0.0)))
+        if k == 0:
+            child = lax.broadcasted_iota(jnp.int32, (16, HD), 1) % rows // per_kv
+            for i in range(beams):
+                stats = jnp.where((which == 3) & (child == i) & (parents[b ^ i] == b), 1.0, stats)
         outs[k][count : count + 16, :] = stats.astype(BF)
+    large.wait()
 
 
 def merge_kernel(ctx_count, beams, heads, kv_count, per_kv, *refs):
@@ -110,6 +148,8 @@
     lses = []
     for k in range(ctx_count):
         line = states[k][count : count + 16, :].astype(F32)
+        if k == 0:
+            mine = jnp.sum(jnp.where(diagonal, line[3:4], 0.0), axis=-1, keepdims=True)
         line = line[0:1] + line[1:2] + line[2:3]
         lses.append(jnp.sum(jnp.where(diagonal, line, 0.0), axis=-1, keepdims=True))
     peak = own
@@ -122,7 +162,7 @@
         weight = jnp.exp(lses[k] - peak)
         total = total + weight
         blended = blended + weight * states[k][0:count, :].astype(F32)
-    result = (blended / total).astype(BF)
+    result = jnp.where(mine > 0.0, blended / total, 0.0).astype(BF)
     for r in range(kv_count):
         for i in range(beams):
             at = r * rows + i * per_kv
@@ -130,31 +170,40 @@
 
 
 def project_kernel(ctx_count, beams, heads, *refs):
-    parents, rows_of, weight = refs[0], refs[1 : 1 + beams], refs[1 + beams]
-    outs, (laid, wide) = refs[2 + beams : 2 + beams + ctx_count], refs[2 + beams + ctx_count :]
-    b = lax.axis_index("beam")
+    rows_of, pieces, w_hbm = refs[:beams], refs[beams : beams + PIECES - 1], refs[beams + PIECES - 1]
+    outs = refs[beams + PIECES : beams + PIECES + ctx_count]
+    last, laid, wide, sem = refs[beams + PIECES + ctx_count :]
+    depth = last.shape[0]
+    copy = pltpu.make_async_copy(w_hbm.at[pl.ds((PIECES - 1) * depth, depth)], last, sem)
+    copy.start()
     c = lax.axis_index("ctx")
     laid[...] = jnp.zeros_like(laid)
     for i in range(beams):
-        source = parents[i] ^ b
         row = rows_of[0][i].astype(F32)
         for k in range(1, beams):
-            row = jnp.where(source == k, rows_of[k][i].astype(F32), row)
+            row = row + rows_of[k][i].astype(F32)
         laid[i * heads : (i + 1) * heads, :] = row
     for h in range(heads):
         wide[:, h * HD : (h + 1) * HD] = laid[pl.ds(h, 8, stride=heads), :].astype(BF)
-    columns = weight.shape[1] // ctx_count
+    columns = last.shape[1] // ctx_count
     step = min(512, columns)
+
+    def share(k, j, n, ref):
+        at = pl.multiple_of((c ^ k) * columns + j * step, 128)
+        return jnp.dot(
+            wide[:, n * depth : (n + 1) * depth], ref[:, pl.ds(at, step)], preferred_element_type=F32
+        )[:beams]
+
     for k in range(ctx_count):
         for j in range(columns // step):
-            at = pl.multiple_of((c ^ k) * columns + j * step, 128)
-            part = jnp.dot(wide[...], weight[:, pl.ds(at, step)], preferred_element_type=F32)
-            outs[k][:, j * step : (j + 1) * step] = part[:beams]
-
-
-def per_device(
-    queries, new_keys, new_values, cache_keys, cache_values, parents, lengths, out_weight
-):
+            outs[k][:, j * step : (j + 1) * step] = sum(share(k, j, n, ref) for n, ref in enumerate(pieces))
+    copy.wait()
+    for k in range(ctx_count):
+        for j in range(columns // step):
+            outs[k][:, j * step : (j + 1) * step] += share(k, j, PIECES - 1, last)
+
+
+def step(queries, new_keys, new_values, cache_keys, cache_values, parents, lengths, out_weight):
     ctx_count = lax.axis_size("ctx")
     beams = lax.axis_size("beam")
     heads = queries.shape[1] // HD
@@ -164,31 +213,53 @@
     packet_rows = -(-(heads + 2 * kv_count) // 16) * 16
     count = beams * heads
 
+    queries, new_keys, new_values, parents, lengths, out_weight = (
+        pltpu.with_memory_space_constraint(x, pltpu.HBM)
+        for x in (queries, new_keys, new_values, parents, lengths, out_weight)
+    )
+    depth = out_weight.shape[0] // PIECES
+    piece = jax.ShapeDtypeStruct((depth, out_weight.shape[1]), BF)
+
+    def fetch(n):
+        return pl.pallas_call(
+            lambda *refs: fetch_kernel(n, *refs),
+            out_shape=piece,
+            in_specs=[HBM],
+            out_specs=VMEM,
+            scratch_shapes=[pltpu.SemaphoreType.DMA],
+            compiler_params=params(4),
+            cost_estimate=cost(0, 2 * piece.size),
+        )(out_weight)
+
     packet = pl.pallas_call(
         lambda *refs: pack_kernel(heads, kv_count, *refs),
         out_shape=jax.ShapeDtypeStruct((packet_rows, HD), BF),
-        in_specs=[VMEM] * 3,
+        in_specs=[HBM] * 3,
         out_specs=VMEM,
-        scratch_shapes=[pltpu.VMEM((packet_rows, HD), F32)],
+        scratch_shapes=[pltpu.VMEM(x.shape, BF) for x in (queries, new_keys, new_values)]
+        + [pltpu.VMEM((packet_rows, HD), F32), pltpu.SemaphoreType.DMA((3,))],
         compiler_params=params(4),
         name="pack",
     )(queries, new_keys, new_values)
     kt = jnp.transpose(cache_keys[0], (1, 0, 2))
     vt = jnp.transpose(cache_values[0], (1, 0, 2))
-    stack = jnp.stack([packet] + [partner(packet, "beam", k) for k in range(1, beams)])
-    stacks = [stack] + [partner(stack, "ctx", k) for k in range(1, ctx_count)]
+    stack = jnp.stack([packet] + partners(packet, "beam"))
+    stacks = [stack] + partners(stack, "ctx")
+    first_piece = fetch(0)
 
     state = jax.ShapeDtypeStruct((count + 16, HD), BF)
-    states = pl.pallas_call(
+    *states, second_piece = pl.pallas_call(
         lambda *refs: attend_kernel(ctx_count, beams, heads, kv_count, per_kv, tokens, *refs),
-        out_shape=[state] * ctx_count,
-        in_specs=[SMEM] + [VMEM] * (ctx_count + 2),
-        out_specs=[VMEM] * ctx_count,
+        out_shape=[state] * ctx_count + [piece],
+        in_specs=[HBM] * 3 + [VMEM] * (ctx_count + 2),
+        out_specs=[VMEM] * (ctx_count + 1),
+        scratch_shapes=[pltpu.SMEM(lengths.shape, jnp.int32)] * 2 + [pltpu.SemaphoreType.DMA((3,))],
         compiler_params=params(8),
-        cost_estimate=cost(4 * beams * H * tokens * HD, 4 * tokens * KVH * HD),
+        cost_estimate=cost(4 * beams * H * tokens * HD, 2 * piece.size),
         name="attend",
-    )(lengths, *stacks, kt, vt)
-    states = [states[0]] + [partner(states[k], "ctx", k) for k in range(1, ctx_count)]
+    )(lengths, parents, out_weight, kt, vt, *stacks)
+    states = [states[0]] + partners(states, "ctx")
+    third_piece = fetch(2)
 
     attended = pl.pallas_call(
         lambda *refs: merge_kernel(ctx_count, beams, heads, kv_count, per_kv, *refs),
@@ -198,22 +269,27 @@
         compiler_params=params(8),
         name="merge",
     )(stack, *states)
-    rows_of = [attended] + [partner(attended, "beam", k) for k in range(1, beams)]
+    rows_of = [attended] + partners(attended, "beam")
 
     columns = out_weight.shape[1] // ctx_count
     parts = pl.pallas_call(
         lambda *refs: project_kernel(ctx_count, beams, heads, *refs),
         out_shape=[jax.ShapeDtypeStruct((beams, columns), F32)] * ctx_count,
-        in_specs=[SMEM] + [VMEM] * (beams + 1),
+        in_specs=[VMEM] * (beams + PIECES - 1) + [HBM],
         out_specs=[VMEM] * ctx_count,
-        scratch_shapes=[pltpu.VMEM((8 * heads, HD), F32), pltpu.VMEM((8, heads * HD), BF)],
-        compiler_params=params(8),
-        cost_estimate=cost(16 * out_weight.size, 2 * out_weight.size),
+        scratch_shapes=[
+            pltpu.VMEM(piece.shape, BF),
+            pltpu.VMEM((8 * heads, HD), F32),
+            pltpu.VMEM((8, heads * HD), BF),
+            pltpu.SemaphoreType.DMA,
+        ],
+        compiler_params=params(16),
+        cost_estimate=cost(16 * out_weight.size, 2 * piece.size),
         name="project",
-    )(parents, *rows_of, out_weight)
+    )(*rows_of, first_piece, second_piece, third_piece, out_weight)
     total = parts[0]
-    for k in range(1, ctx_count):
-        total = total + partner(parts[k], "ctx", k)
+    for part in partners(parts, "ctx"):
+        total = total + part
     return total.astype(BF)
 
 
@@ -229,7 +305,7 @@
         P("ctx", "beam"),
     )
     return jax.shard_map(
-        per_device,
+        step,
         mesh=mesh,
         in_specs=placed,
         out_specs=P("groups", ("beam", "ctx")),

time: 53.7 us -> 47.8 us (0.89)
  local copies, waits for them, and re-layouts: 15.9 us -> 1.92 us
  Pallas kernels: 8.24 us -> 18.4 us
  waiting for transfers between devices: 12.6 us -> 10.4 us
    unnamed x12 -> x0, local copies, waits for them, and re-layouts: 13.9 us -> none
    pallas_call x4 -> x6, Pallas kernels: 8.24 us -> 18.4 us  [the longest x1 7.04 us: step(): pl.pallas_call(lambda *refs: project_kernel(ctx_count, beams, heads, *ref...]
    ppermute x15, waiting for transfers between devices: 12.6 us -> 10.4 us  [partners(): found.append(lax.ppermute(array, axis, [(i, i ^ k) for i in range(length)]))]
  transfers between devices with their start and end apart: 15 -> 15, of which waited for: 11 -> 8; matrix products, arithmetic and copies ran while one was open for 4% -> 4% of each run, Pallas kernels for 0% -> 14%
where the time goes in v2:
time: 47.8 us; the launch traced here: 47.5 us
  Pallas kernels  18.4 us (38%)
  starting transfers between devices  16 us (33%)
  waiting for transfers between devices  10.4 us (22%)
  local copies, waits for them, and re-layouts  1.92 us (4%)
  other arithmetic  0.62 us (1%)
    ppermute x15, starting transfers between devices, partners(): found.append(lax.ppermute(array, axis, [(i, i ^ k) for i in range(length)]))  16 us
    ppermute x15, waiting for transfers between devices, partners(): found.append(lax.ppermute(array, axis, [(i, i ^ k) for i in range(length)]))  10.4 us
    pallas_call x1, Pallas kernels, step(): pl.pallas_call(lambda *refs: project_kernel(ctx_count, beams, heads, *ref...  7.04 us
    pallas_call x2, Pallas kernels, fetch(): pl.pallas_call(lambda *refs: fetch_kernel(n, *refs), out_shape=piece, in_...  6.78 us
    pallas_call x1, Pallas kernels, step(): pl.pallas_call(lambda *refs: attend_kernel(ctx_count, beams, heads, kv_co...  3.41 us
    transpose x1, local copies, waits for them, and re-layouts, step(): vt = jnp.transpose(cache_values[0], (1, 0, 2))  1.92 us
  transfers between devices with their start and end apart: 15, of which 8 were waited for; matrix products, arithmetic and copies ran while one was open for 4% of the time, Pallas kernels for 14%

profile of v2, /device:TPU:0, one launch (start us, length us, event | category | flops | bytes accessed | tf_op | source)
XLA Modules:
  0.0 47.5 jit_solution(5112264221534329202)
XLA Ops:
  0.0 0.8 %pack.1 = bf16[48,128]{1,0:T(8,128)(2,1)S(1)} custom-call(bf16[1,4096]{1,0:T(2,128)(2,1)} %refs_0_.4, bf16[1,1024]{1,0:T(2,128)(2,1)} %refs_1_.2, bf16[1,1024]{1,0:T(2,128)(2,1)} %refs_2_.2), custom_call_target="tpu_custom_call" | custom-call | tf_op jit(solution)/shard_map/pack/pallas_call | solution.py:234
  0.8 5.1 %collective-permute-start.2 = (bf16[48,128]{1,0:T(8,128)(2,1)S(1)}, bf16[48,128]{1,0:T(8,128)(2,1)S(1)}, u32[]{:S(2)}, u32[]{:S(2)}) collective-permute-start(bf16[48,128]{1,0:T(8,128)(2,1)S(1)} %pack.1), channel_id=1, source_target_pairs={{0,12},{4,8},{8,4},{12,0},{1,13},{5,9},{9,5},{13,1},{2,14},{6,10},... | collective-permute-start | bytes 36872 | tf_op jit(solution)/shard_map/ppermute | solution.py:40
  5.9 0.0 collective-permute-start.1
  5.9 0.6 %collective-permute-start = (bf16[48,128]{1,0:T(8,128)(2,1)S(1)}, bf16[48,128]{1,0:T(8,128)(2,1)S(1)}, u32[]{:S(2)}, u32[]{:S(2)}) collective-permute-start(bf16[48,128]{1,0:T(8,128)(2,1)S(1)} %pack.1), channel_id=1, source_target_pairs={{0,4},{4,0},{8,12},{12,8},{1,5},{5,1},{9,13},{13,9},{2,6},{6,2},{1... | collective-permute-start | bytes 36872 | tf_op jit(solution)/shard_map/ppermute | solution.py:40
  6.6 1.0 %collective-permute-done.2 = bf16[48,128]{1,0:T(8,128)(2,1)S(1)} collective-permute-done((bf16[48,128]{1,0:T(8,128)(2,1)S(1)}, bf16[48,128]{1,0:T(8,128)(2,1)S(1)}, u32[]{:S(2)}, u32[]{:S(2)}) %collective-permute-start.2) | collective-permute-done | bytes 12320 | tf_op jit(solution)/shard_map/ppermute | solution.py:40
  7.6 2.9 %collective-permute-done.1 = bf16[48,128]{1,0:T(8,128)(2,1)S(1)} collective-permute-done((bf16[48,128]{1,0:T(8,128)(2,1)S(1)}, bf16[48,128]{1,0:T(8,128)(2,1)S(1)}, u32[]{:S(2)}, u32[]{:S(2)}) %collective-permute-start.1) | collective-permute-done | bytes 12320 | tf_op jit(solution)/shard_map/ppermute | solution.py:40
  10.5 0.1 collective-permute-start.5
  10.6 1.6 %collective-permute-start.4 = (bf16[4,48,128]{2,1,0:T(8,128)(2,1)S(1)}, bf16[4,48,128]{2,1,0:T(8,128)(2,1)S(1)}, u32[]{:S(2)}, u32[]{:S(2)}) collective-permute-start(bf16[4,48,128]{2,1,0:T(8,128)(2,1)S(1)} %pad_maximum_fusion.refs_5_.refs_0_), channel_id=1, source_target_pairs={{0,2},{1,3},{2,0},{3,1},{4,6},{5,7},{6,4},{7,5},{8,10},{9,11},{10,... | collective-permute-start | bytes 147464 | tf_op jit(solution)/shard_map/ppermute | solution.py:40
  12.2 0.3 collective-permute-start.3
  12.5 1.9 %copy_bitcast_fusion = (bf16[8,512,128]{2,1,0:T(8,128)(2,1)S(1)}, bf16[8,512,128]{2,1,0:T(8,128)(2,1)S(1)}) fusion(bf16[1,512,8,128]{3,2,1,0:T(8,128)(2,1)} %param.12, bf16[1,512,8,128]{3,2,1,0:T(8,128)(2,1)} %param.11), kind=kLoop, calls=%fused_computation | loop fusion | bytes 4194304 | tf_op jit(solution)/shard_map/transpose | solution.py:245
  14.4 0.2 collective-permute-done.5.refs_8_
  14.6 0.9 %collective-permute-done.4.refs_7_ = bf16[4,48,128]{2,1,0:T(8,128)(2,1)S(1)} collective-permute-done((bf16[4,48,128]{2,1,0:T(8,128)(2,1)S(1)}, bf16[4,48,128]{2,1,0:T(8,128)(2,1)S(1)}, u32[]{:S(2)}, u32[]{:S(2)}) %collective-permute-start.4) | collective-permute-done | bytes 49184 | tf_op jit(solution)/shard_map/ppermute | solution.py:40
  15.5 3.4 %attend.1 = (bf16[144,128]{1,0:T(8,128)(2,1)S(1)}, bf16[144,128]{1,0:T(8,128)(2,1)S(1)}, bf16[144,128]{1,0:T(8,128)(2,1)S(1)}, bf16[144,128]{1,0:T(8,128)(2,1)S(1)}, bf16[1024,4096]{1,0:T(8,128)(2,1)S(1)}) custom-call(s32[4]{0:T(128)} %refs_0_.5, s32[4]{0:T(128)} %refs_1_.3, bf16[4096,4096]{1,0:T(8,128)(2,1)} %refs_7_.1, ...), custom_call_target="tpu_custom_call" | custom-call | flops 134217728 | bytes 8388608 | tf_op jit(solution)/shard_map/attend/pallas_call | solution.py:251
  18.9 0.2 collective-permute-start.6
  19.1 1.1 %collective-permute-start.7 = (bf16[144,128]{1,0:T(8,128)(2,1)S(1)}, bf16[144,128]{1,0:T(8,128)(2,1)S(1)}, u32[]{:S(2)}, u32[]{:S(2)}) collective-permute-start(bf16[144,128]{1,0:T(8,128)(2,1)S(1)} %get-tuple-element.16), channel_id=1, source_target_pairs={{0,2},{1,3},{2,0},{3,1},{4,6},{5,7},{6,4},{7,5},{8,10},{9,11},{10,... | collective-permute-start | bytes 110600 | tf_op jit(solution)/shard_map/ppermute | solution.py:40
  20.3 0.6 %collective-permute-start.8 = (bf16[144,128]{1,0:T(8,128)(2,1)S(1)}, bf16[144,128]{1,0:T(8,128)(2,1)S(1)}, u32[]{:S(2)}, u32[]{:S(2)}) collective-permute-start(bf16[144,128]{1,0:T(8,128)(2,1)S(1)} %get-tuple-element.17), channel_id=1, source_target_pairs={{0,3},{1,2},{2,1},{3,0},{4,7},{5,6},{6,5},{7,4},{8,11},{9,10},{10,... | collective-permute-start | bytes 110600 | tf_op jit(solution)/shard_map/ppermute | solution.py:40
  20.9 2.2 %collective-permute-done.7.refs_3_ = bf16[144,128]{1,0:T(8,128)(2,1)S(1)} collective-permute-done((bf16[144,128]{1,0:T(8,128)(2,1)S(1)}, bf16[144,128]{1,0:T(8,128)(2,1)S(1)}, u32[]{:S(2)}, u32[]{:S(2)}) %collective-permute-start.7) | collective-permute-done | bytes 36896 | tf_op jit(solution)/shard_map/ppermute | solution.py:40
  23.1 0.6 %collective-permute-done.8.refs_4_ = bf16[144,128]{1,0:T(8,128)(2,1)S(1)} collective-permute-done((bf16[144,128]{1,0:T(8,128)(2,1)S(1)}, bf16[144,128]{1,0:T(8,128)(2,1)S(1)}, u32[]{:S(2)}, u32[]{:S(2)}) %collective-permute-start.8) | collective-permute-done | bytes 36896 | tf_op jit(solution)/shard_map/ppermute | solution.py:40
  23.7 0.4 merge.1.refs_0_
  24.1 1.5 %collective-permute-start.11 = (bf16[4,32,128]{2,1,0:T(8,128)(2,1)S(1)}, bf16[4,32,128]{2,1,0:T(8,128)(2,1)S(1)}, u32[]{:S(2)}, u32[]{:S(2)}) collective-permute-start(bf16[4,32,128]{2,1,0:T(8,128)(2,1)S(1)} %merge.1.refs_0_), channel_id=1, source_target_pairs={{0,12},{4,8},{8,4},{12,0},{1,13},{5,9},{9,5},{13,1},{2,14},{6,10},... | collective-permute-start | bytes 98312 | tf_op jit(solution)/shard_map/ppermute | solution.py:40
  25.6 0.6 %collective-permute-start.10 = (bf16[4,32,128]{2,1,0:T(8,128)(2,1)S(1)}, bf16[4,32,128]{2,1,0:T(8,128)(2,1)S(1)}, u32[]{:S(2)}, u32[]{:S(2)}) collective-permute-start(bf16[4,32,128]{2,1,0:T(8,128)(2,1)S(1)} %merge.1.refs_0_), channel_id=1, source_target_pairs={{0,8},{4,12},{8,0},{12,4},{1,9},{5,13},{9,1},{13,5},{2,10},{6,14},... | collective-permute-start | bytes 98312 | tf_op jit(solution)/shard_map/ppermute | solution.py:40
  26.3 2.3 %collective-permute-start.9 = (bf16[4,32,128]{2,1,0:T(8,128)(2,1)S(1)}, bf16[4,32,128]{2,1,0:T(8,128)(2,1)S(1)}, u32[]{:S(2)}, u32[]{:S(2)}) collective-permute-start(bf16[4,32,128]{2,1,0:T(8,128)(2,1)S(1)} %merge.1.refs_0_), channel_id=1, source_target_pairs={{0,4},{4,0},{8,12},{12,8},{1,5},{5,1},{9,13},{13,9},{2,6},{6,2},{1... | collective-permute-start | bytes 98312 | tf_op jit(solution)/shard_map/ppermute | solution.py:40
  28.6 3.4 %shard_map.82.refs_4_ = bf16[1024,4096]{1,0:T(8,128)(2,1)S(1)} custom-call(bf16[4096,4096]{1,0:T(8,128)(2,1)} %refs_7_.1), custom_call_target="tpu_custom_call" | custom-call | bytes 8388608 | tf_op jit(solution)/shard_map/pallas_call | solution.py:224
  32.0 3.4 %shard_map.83.refs_6_ = bf16[1024,4096]{1,0:T(8,128)(2,1)S(1)} custom-call(bf16[4096,4096]{1,0:T(8,128)(2,1)} %refs_7_.1), custom_call_target="tpu_custom_call" | custom-call | bytes 8388608 | tf_op jit(solution)/shard_map/pallas_call | solution.py:224
  35.4 0.0 collective-permute-done.9.refs_1_
  35.4 7.0 %project.1 = (f32[4,1024]{1,0:T(4,128)S(1)}, f32[4,1024]{1,0:T(4,128)S(1)}, f32[4,1024]{1,0:T(4,128)S(1)}, f32[4,1024]{1,0:T(4,128)S(1)}) custom-call(bf16[4,32,128]{2,1,0:T(8,128)(2,1)S(1)} %merge.1.refs_0_, bf16[4,32,128]{2,1,0:T(8,128)(2,1)S(1)} %collective-permute-done.9.refs_1_, bf16[4,32,128]{2,1,0:T(8,128)(2,1)S(1)} %collective-permute-done.10.refs_2_, ...), custom_call_target="tpu_custom_call" | custom-call | flops 268435456 | bytes 8388608 | tf_op jit(solution)/shard_map/project/pallas_call | solution.py:275
  42.4 0.1 collective-permute-start.12
  42.5 1.2 %collective-permute-start.13 = (f32[4,1024]{1,0:T(4,128)S(1)}, f32[4,1024]{1,0:T(4,128)S(1)}, u32[]{:S(2)}, u32[]{:S(2)}) collective-permute-start(f32[4,1024]{1,0:T(4,128)S(1)} %get-tuple-element.21), channel_id=1, source_target_pairs={{0,2},{1,3},{2,0},{3,1},{4,6},{5,7},{6,4},{7,5},{8,10},{9,11},{10,... | collective-permute-start | bytes 49160 | tf_op jit(solution)/shard_map/ppermute | solution.py:40
  43.7 0.7 %collective-permute-start.14 = (f32[4,1024]{1,0:T(4,128)S(1)}, f32[4,1024]{1,0:T(4,128)S(1)}, u32[]{:S(2)}, u32[]{:S(2)}) collective-permute-start(f32[4,1024]{1,0:T(4,128)S(1)} %get-tuple-element.22), channel_id=1, source_target_pairs={{0,3},{1,2},{2,1},{3,0},{4,7},{5,6},{6,5},{7,4},{8,11},{9,10},{10,... | collective-permute-start | bytes 49160 | tf_op jit(solution)/shard_map/ppermute | solution.py:40
  44.4 2.0 %collective-permute-done.13 = f32[4,1024]{1,0:T(4,128)S(1)} collective-permute-done((f32[4,1024]{1,0:T(4,128)S(1)}, f32[4,1024]{1,0:T(4,128)S(1)}, u32[]{:S(2)}, u32[]{:S(2)}) %collective-permute-start.13) | collective-permute-done | bytes 16416 | tf_op jit(solution)/shard_map/ppermute | solution.py:40
  46.3 0.5 %collective-permute-done.14 = f32[4,1024]{1,0:T(4,128)S(1)} collective-permute-done((f32[4,1024]{1,0:T(4,128)S(1)}, f32[4,1024]{1,0:T(4,128)S(1)}, u32[]{:S(2)}, u32[]{:S(2)}) %collective-permute-start.14) | collective-permute-done | bytes 16416 | tf_op jit(solution)/shard_map/ppermute | solution.py:40
  46.8 0.6 %add_convert_fusion = bf16[4,1024]{1,0:T(4,128)(2,1)} fusion(f32[4,1024]{1,0:T(4,128)S(1)} %collective-permute-done.14, f32[4,1024]{1,0:T(4,128)S(1)} %collective-permute-done.13, f32[4,1024]{1,0:T(4,128)S(1)} %get-tuple-element.19, f32[4,1024]{1,0:T(4,128)S(1)} %collective-permute-done.12), kind=kLoop, calls=%fused_computation.3 | loop fusion | flops 16384 | bytes 73728 | tf_op jit(solution)/shard_map/convert_element_type | solution.py:293
  (7 shorter events, 0.0 us)
Async XLA Ops:
  0.8 6.8 %collective-permute-start.2 = (bf16[48,128]{1,0:T(8,128)(2,1)S(1)}, bf16[48,128]{1,0:T(8,128)(2,1)S(1)}, u32[]{:S(2)}, u32[]{:S(2)}) collective-permute-start(bf16[48,128]{1,0:T(8,128)(2,1)S(1)} %pack.1), channel_id=1, source_target_pairs={{0,12},{4,8},{8,4},{12,0},{1,13},{5,9},{9,5},{13,1},{2,14},{6,10},... | collective-permute-start | bytes 36872 | tf_op jit(solution)/shard_map/ppermute | solution.py:40
  5.9 4.6 %collective-permute-start.1 = (bf16[48,128]{1,0:T(8,128)(2,1)S(1)}, bf16[48,128]{1,0:T(8,128)(2,1)S(1)}, u32[]{:S(2)}, u32[]{:S(2)}) collective-permute-start(bf16[48,128]{1,0:T(8,128)(2,1)S(1)} %pack.1), channel_id=1, source_target_pairs={{0,8},{4,12},{8,0},{12,4},{1,9},{5,13},{9,1},{13,5},{2,10},{6,14},... | collective-permute-start | bytes 36872 | tf_op jit(solution)/shard_map/ppermute | solution.py:40
  5.9 4.6 %collective-permute-start = (bf16[48,128]{1,0:T(8,128)(2,1)S(1)}, bf16[48,128]{1,0:T(8,128)(2,1)S(1)}, u32[]{:S(2)}, u32[]{:S(2)}) collective-permute-start(bf16[48,128]{1,0:T(8,128)(2,1)S(1)} %pack.1), channel_id=1, source_target_pairs={{0,4},{4,0},{8,12},{12,8},{1,5},{5,1},{9,13},{13,9},{2,6},{6,2},{1... | collective-permute-start | bytes 36872 | tf_op jit(solution)/shard_map/ppermute | solution.py:40
  10.5 4.0 %collective-permute-start.5 = (bf16[4,48,128]{2,1,0:T(8,128)(2,1)S(1)}, bf16[4,48,128]{2,1,0:T(8,128)(2,1)S(1)}, u32[]{:S(2)}, u32[]{:S(2)}) collective-permute-start(bf16[4,48,128]{2,1,0:T(8,128)(2,1)S(1)} %pad_maximum_fusion.refs_5_.refs_0_), channel_id=1, source_target_pairs={{0,3},{1,2},{2,1},{3,0},{4,7},{5,6},{6,5},{7,4},{8,11},{9,10},{10,... | collective-permute-start | bytes 147464 | tf_op jit(solution)/shard_map/ppermute | solution.py:40
  10.6 4.9 %collective-permute-start.4 = (bf16[4,48,128]{2,1,0:T(8,128)(2,1)S(1)}, bf16[4,48,128]{2,1,0:T(8,128)(2,1)S(1)}, u32[]{:S(2)}, u32[]{:S(2)}) collective-permute-start(bf16[4,48,128]{2,1,0:T(8,128)(2,1)S(1)} %pad_maximum_fusion.refs_5_.refs_0_), channel_id=1, source_target_pairs={{0,2},{1,3},{2,0},{3,1},{4,6},{5,7},{6,4},{7,5},{8,10},{9,11},{10,... | collective-permute-start | bytes 147464 | tf_op jit(solution)/shard_map/ppermute | solution.py:40
  12.2 3.3 %collective-permute-start.3 = (bf16[4,48,128]{2,1,0:T(8,128)(2,1)S(1)}, bf16[4,48,128]{2,1,0:T(8,128)(2,1)S(1)}, u32[]{:S(2)}, u32[]{:S(2)}) collective-permute-start(bf16[4,48,128]{2,1,0:T(8,128)(2,1)S(1)} %pad_maximum_fusion.refs_5_.refs_0_), channel_id=1, source_target_pairs={{0,1},{1,0},{2,3},{3,2},{4,5},{5,4},{6,7},{7,6},{8,9},{9,8},{10,11... | collective-permute-start | bytes 147464 | tf_op jit(solution)/shard_map/ppermute | solution.py:40
  18.9 1.9 %collective-permute-start.6 = (bf16[144,128]{1,0:T(8,128)(2,1)S(1)}, bf16[144,128]{1,0:T(8,128)(2,1)S(1)}, u32[]{:S(2)}, u32[]{:S(2)}) collective-permute-start(bf16[144,128]{1,0:T(8,128)(2,1)S(1)} %get-tuple-element.15), channel_id=1, source_target_pairs={{0,1},{1,0},{2,3},{3,2},{4,5},{5,4},{6,7},{7,6},{8,9},{9,8},{10,11... | collective-permute-start | bytes 110600 | tf_op jit(solution)/shard_map/ppermute | solution.py:40
  19.1 4.0 %collective-permute-start.7 = (bf16[144,128]{1,0:T(8,128)(2,1)S(1)}, bf16[144,128]{1,0:T(8,128)(2,1)S(1)}, u32[]{:S(2)}, u32[]{:S(2)}) collective-permute-start(bf16[144,128]{1,0:T(8,128)(2,1)S(1)} %get-tuple-element.16), channel_id=1, source_target_pairs={{0,2},{1,3},{2,0},{3,1},{4,6},{5,7},{6,4},{7,5},{8,10},{9,11},{10,... | collective-permute-start | bytes 110600 | tf_op jit(solution)/shard_map/ppermute | solution.py:40
  20.3 3.4 %collective-permute-start.8 = (bf16[144,128]{1,0:T(8,128)(2,1)S(1)}, bf16[144,128]{1,0:T(8,128)(2,1)S(1)}, u32[]{:S(2)}, u32[]{:S(2)}) collective-permute-start(bf16[144,128]{1,0:T(8,128)(2,1)S(1)} %get-tuple-element.17), channel_id=1, source_target_pairs={{0,3},{1,2},{2,1},{3,0},{4,7},{5,6},{6,5},{7,4},{8,11},{9,10},{10,... | collective-permute-start | bytes 110600 | tf_op jit(solution)/shard_map/ppermute | solution.py:40
  24.1 11.3 %collective-permute-start.11 = (bf16[4,32,128]{2,1,0:T(8,128)(2,1)S(1)}, bf16[4,32,128]{2,1,0:T(8,128)(2,1)S(1)}, u32[]{:S(2)}, u32[]{:S(2)}) collective-permute-start(bf16[4,32,128]{2,1,0:T(8,128)(2,1)S(1)} %merge.1.refs_0_), channel_id=1, source_target_pairs={{0,12},{4,8},{8,4},{12,0},{1,13},{5,9},{9,5},{13,1},{2,14},{6,10},... | collective-permute-start | bytes 98312 | tf_op jit(solution)/shard_map/ppermute | solution.py:40
  25.6 9.7 %collective-permute-start.10 = (bf16[4,32,128]{2,1,0:T(8,128)(2,1)S(1)}, bf16[4,32,128]{2,1,0:T(8,128)(2,1)S(1)}, u32[]{:S(2)}, u32[]{:S(2)}) collective-permute-start(bf16[4,32,128]{2,1,0:T(8,128)(2,1)S(1)} %merge.1.refs_0_), channel_id=1, source_target_pairs={{0,8},{4,12},{8,0},{12,4},{1,9},{5,13},{9,1},{13,5},{2,10},{6,14},... | collective-permute-start | bytes 98312 | tf_op jit(solution)/shard_map/ppermute | solution.py:40
  26.3 9.1 %collective-permute-start.9 = (bf16[4,32,128]{2,1,0:T(8,128)(2,1)S(1)}, bf16[4,32,128]{2,1,0:T(8,128)(2,1)S(1)}, u32[]{:S(2)}, u32[]{:S(2)}) collective-permute-start(bf16[4,32,128]{2,1,0:T(8,128)(2,1)S(1)} %merge.1.refs_0_), channel_id=1, source_target_pairs={{0,4},{4,0},{8,12},{12,8},{1,5},{5,1},{9,13},{13,9},{2,6},{6,2},{1... | collective-permute-start | bytes 98312 | tf_op jit(solution)/shard_map/ppermute | solution.py:40
  42.4 1.9 %collective-permute-start.12 = (f32[4,1024]{1,0:T(4,128)S(1)}, f32[4,1024]{1,0:T(4,128)S(1)}, u32[]{:S(2)}, u32[]{:S(2)}) collective-permute-start(f32[4,1024]{1,0:T(4,128)S(1)} %get-tuple-element.20), channel_id=1, source_target_pairs={{0,1},{1,0},{2,3},{3,2},{4,5},{5,4},{6,7},{7,6},{8,9},{9,8},{10,11... | collective-permute-start | bytes 49160 | tf_op jit(solution)/shard_map/ppermute | solution.py:40
  42.5 3.8 %collective-permute-start.13 = (f32[4,1024]{1,0:T(4,128)S(1)}, f32[4,1024]{1,0:T(4,128)S(1)}, u32[]{:S(2)}, u32[]{:S(2)}) collective-permute-start(f32[4,1024]{1,0:T(4,128)S(1)} %get-tuple-element.21), channel_id=1, source_target_pairs={{0,2},{1,3},{2,0},{3,1},{4,6},{5,7},{6,4},{7,5},{8,10},{9,11},{10,... | collective-permute-start | bytes 49160 | tf_op jit(solution)/shard_map/ppermute | solution.py:40
  43.7 3.2 %collective-permute-start.14 = (f32[4,1024]{1,0:T(4,128)S(1)}, f32[4,1024]{1,0:T(4,128)S(1)}, u32[]{:S(2)}, u32[]{:S(2)}) collective-permute-start(f32[4,1024]{1,0:T(4,128)S(1)} %get-tuple-element.22), channel_id=1, source_target_pairs={{0,3},{1,2},{2,1},{3,0},{4,7},{5,6},{6,5},{7,4},{8,11},{9,10},{10,... | collective-permute-start | bytes 49160 | tf_op jit(solution)/shard_map/ppermute | solution.py:40

commit v3 on v2

--- a/solution.py
+++ b/solution.py
@@ -21,7 +21,7 @@
 F32 = jnp.float32
 VMEM = pl.BlockSpec(memory_space=pltpu.VMEM)
 HBM = pl.BlockSpec(memory_space=pltpu.HBM)
-PIECES = 4
+SHARES = (4, 8, 4, 10, 6)
 
 
 def params(mib):
@@ -61,9 +61,8 @@
     out_ref[...] = rows[...].astype(BF)
 
 
-def fetch_kernel(piece, w_hbm, out_ref, sem):
-    rows = out_ref.shape[0]
-    copy = pltpu.make_async_copy(w_hbm.at[pl.ds(piece * rows, rows)], out_ref, sem)
+def fetch_kernel(start, w_hbm, out_ref, sem):
+    copy = pltpu.make_async_copy(w_hbm.at[pl.ds(start, out_ref.shape[0])], out_ref, sem)
     copy.start()
     copy.wait()
 
@@ -81,52 +80,65 @@
     return lax.broadcasted_iota(jnp.int32, shape, 0) == lax.broadcasted_iota(jnp.int32, shape, 1)
 
 
-def attend_kernel(ctx_count, beams, heads, kv_count, per_kv, tokens, *refs):
+def attend_kernel(slots, start, beams, heads, kv_count, per_kv, tokens, *refs):
+    n = len(slots)
     lengths_hbm, parents_hbm, w_hbm, kt, vt = refs[:5]
-    stacks, outs = refs[5 : 5 + ctx_count], refs[5 + ctx_count : 5 + 2 * ctx_count]
-    piece, lengths, parents, sems = refs[5 + 2 * ctx_count :]
+    stacks, outs = refs[5 : 5 + n], refs[5 + n : 5 + 2 * n]
+    piece, lengths, parents, sems = refs[5 + 2 * n :]
     small = [
         pltpu.make_async_copy(lengths_hbm, lengths, sems.at[0]),
         pltpu.make_async_copy(parents_hbm, parents, sems.at[1]),
     ]
-    large = pltpu.make_async_copy(w_hbm.at[pl.ds(piece.shape[0], piece.shape[0])], piece, sems.at[2])
+    large = pltpu.make_async_copy(w_hbm.at[pl.ds(start, piece.shape[0])], piece, sems.at[2])
     for copy in small:
         copy.start()
     large.start()
     b = lax.axis_index("beam")
     c = lax.axis_index("ctx")
+    rows = beams * per_kv
+    count = kv_count * rows
+    pairs = [(i, r) for i in range(n) for r in range(kv_count)]
+
+    def kv_head(i, r):
+        return (c ^ slots[i]) * heads // GROUP + r
+
+    scores = []
+    for i, r in pairs:
+        q = stacks[i][:, r * per_kv : (r + 1) * per_kv, :].astype(F32)
+        q = q.reshape(rows, HD).astype(BF)
+        scores.append(
+            lax.dot_general(q, kt[kv_head(i, r)], (((1,), (1,)), ((), ())), preferred_element_type=F32)
+        )
     for copy in small:
         copy.wait()
     limit = lengths[b] * SPAN - c * tokens
-    rows = beams * per_kv
     keep = lax.broadcasted_iota(jnp.int32, (rows, tokens), 1) < limit
-    for k in range(ctx_count):
-        first = (c ^ k) * heads // GROUP
-        lses = []
-        for r in range(kv_count):
-            q = stacks[k][:, r * per_kv : (r + 1) * per_kv, :].astype(F32)
-            q = q.reshape(rows, HD).astype(BF)
-            s = lax.dot_general(q, kt[first + r], (((1,), (1,)), ((), ())), preferred_element_type=F32)
-            s = jnp.where(keep, s * SCALE, MASKED)
-            peak = jnp.max(s, axis=-1, keepdims=True)
-            w = jnp.where(keep, jnp.exp(s - peak), 0.0)
-            total = jnp.sum(w, axis=-1, keepdims=True)
-            o = jnp.dot(w.astype(BF), vt[first + r], preferred_element_type=F32)
-            some = total > 0.0
-            safe = jnp.where(some, total, 1.0)
-            outs[k][r * rows : (r + 1) * rows, :] = (o / safe).astype(BF)
-            lses.append(jnp.where(some, peak + jnp.log(safe), MASKED))
-        lse = jnp.concatenate(lses, axis=0) if kv_count > 1 else lses[0]
-        count = kv_count * rows
-        line = jnp.sum(jnp.where(eye(count), lse, 0.0), axis=0, keepdims=True)
+    scores = [jnp.where(keep, s * SCALE, MASKED) for s in scores]
+    peaks = [jnp.max(s, axis=-1, keepdims=True) for s in scores]
+    weights = [jnp.where(keep, jnp.exp(s - m), 0.0) for s, m in zip(scores, peaks)]
+    totals = [jnp.sum(w, axis=-1, keepdims=True) for w in weights]
+    blended = [
+        jnp.dot(w.astype(BF), vt[kv_head(i, r)], preferred_element_type=F32)
+        for w, (i, r) in zip(weights, pairs)
+    ]
+    safe = [jnp.where(t > 0.0, t, 1.0) for t in totals]
+    lses = [jnp.where(t > 0.0, m + jnp.log(f), MASKED) for t, m, f in zip(totals, peaks, safe)]
+    which = lax.broadcasted_iota(jnp.int32, (16, HD), 0)
+    diagonal = eye(count)
+    for i in range(n):
+        mine = slice(i * kv_count, (i + 1) * kv_count)
+        outs[i][0:count, :] = jnp.concatenate(
+            [(o / f).astype(BF) for o, f in zip(blended[mine], safe[mine])], axis=0
+        )
+        lse = jnp.concatenate(lses[mine], axis=0)
+        line = jnp.sum(jnp.where(diagonal, lse, 0.0), axis=0, keepdims=True)
         parts = [p.astype(F32) for p in split3(line)]
-        which = lax.broadcasted_iota(jnp.int32, (16, HD), 0)
         stats = jnp.where(which == 0, parts[0], jnp.where(which == 1, parts[1], jnp.where(which == 2, parts[2], 0.0)))
-        if k == 0:
+        if slots[i] == 0:
             child = lax.broadcasted_iota(jnp.int32, (16, HD), 1) % rows // per_kv
-            for i in range(beams):
-                stats = jnp.where((which == 3) & (child == i) & (parents[b ^ i] == b), 1.0, stats)
-        outs[k][count : count + 16, :] = stats.astype(BF)
+            for k in range(beams):
+                stats = jnp.where((which == 3) & (child == k) & (parents[b ^ k] == b), 1.0, stats)
+        outs[i][count : count + 16, :] = stats.astype(BF)
     large.wait()
 
 
@@ -169,12 +181,17 @@
             out_ref[b ^ i, r * per_kv : (r + 1) * per_kv, :] = result[at : at + per_kv, :]
 
 
-def project_kernel(ctx_count, beams, heads, *refs):
-    rows_of, pieces, w_hbm = refs[:beams], refs[beams : beams + PIECES - 1], refs[beams + PIECES - 1]
-    outs = refs[beams + PIECES : beams + PIECES + ctx_count]
-    last, laid, wide, sem = refs[beams + PIECES + ctx_count :]
-    depth = last.shape[0]
-    copy = pltpu.make_async_copy(w_hbm.at[pl.ds((PIECES - 1) * depth, depth)], last, sem)
+def chunk(rows, pieces, bounds, beams, at, width):
+    return sum(
+        jnp.dot(rows[:, lo:hi], ref[:, pl.ds(at, width)], preferred_element_type=F32)
+        for ref, lo, hi in zip(pieces, bounds, bounds[1:])
+    )[:beams]
+
+
+def project_kernel(ctx_count, beams, heads, bounds, *refs):
+    rows_of, pieces, w_hbm = refs[:beams], refs[beams : beams + 4], refs[beams + 4]
+    outs, (last, wide), (laid, sem) = refs[beams + 5 : -4], refs[-4:-2], refs[-2:]
+    copy = pltpu.make_async_copy(w_hbm.at[pl.ds(bounds[4], last.shape[0])], last, sem)
     copy.start()
     c = lax.axis_index("ctx")
     laid[...] = jnp.zeros_like(laid)
@@ -186,21 +203,24 @@
     for h in range(heads):
         wide[:, h * HD : (h + 1) * HD] = laid[pl.ds(h, 8, stride=heads), :].astype(BF)
     columns = last.shape[1] // ctx_count
-    step = min(512, columns)
-
-    def share(k, j, n, ref):
-        at = pl.multiple_of((c ^ k) * columns + j * step, 128)
-        return jnp.dot(
-            wide[:, n * depth : (n + 1) * depth], ref[:, pl.ds(at, step)], preferred_element_type=F32
-        )[:beams]
-
-    for k in range(ctx_count):
-        for j in range(columns // step):
-            outs[k][:, j * step : (j + 1) * step] = sum(share(k, j, n, ref) for n, ref in enumerate(pieces))
+    width = min(512, columns)
+    places = [(k, j) for k in range(1, ctx_count) for j in range(0, columns, width)]
+    for k, j in places:
+        at = pl.multiple_of((c ^ k) * columns + j, 128)
+        outs[k - 1][:, j : j + width] = chunk(wide, pieces, bounds[:5], beams, at, width)
     copy.wait()
-    for k in range(ctx_count):
-        for j in range(columns // step):
-            outs[k][:, j * step : (j + 1) * step] += share(k, j, PIECES - 1, last)
+    for k, j in places:
+        at = pl.multiple_of((c ^ k) * columns + j, 128)
+        outs[k - 1][:, j : j + width] += chunk(wide, [last], bounds[4:], beams, at, width)
+
+
+def home_kernel(ctx_count, beams, bounds, wide, *refs):
+    pieces, out_ref = refs[:-1], refs[-1]
+    columns = pieces[0].shape[1] // ctx_count
+    width = min(512, columns)
+    for j in range(0, columns, width):
+        at = pl.multiple_of(lax.axis_index("ctx") * columns + j, 128)
+        out_ref[:, j : j + width] = chunk(wide, pieces, bounds, beams, at, width)
 
 
 def step(queries, new_keys, new_values, cache_keys, cache_values, parents, lengths, out_weight):
@@ -217,19 +237,30 @@
         pltpu.with_memory_space_constraint(x, pltpu.HBM)
         for x in (queries, new_keys, new_values, parents, lengths, out_weight)
     )
-    depth = out_weight.shape[0] // PIECES
-    piece = jax.ShapeDtypeStruct((depth, out_weight.shape[1]), BF)
+    bounds = [heads * sum(SHARES[:n]) // sum(SHARES) * HD for n in range(len(SHARES) + 1)]
+    piece = [jax.ShapeDtypeStruct((hi - lo, out_weight.shape[1]), BF) for lo, hi in zip(bounds, bounds[1:])]
 
     def fetch(n):
         return pl.pallas_call(
-            lambda *refs: fetch_kernel(n, *refs),
-            out_shape=piece,
+            lambda *refs: fetch_kernel(bounds[n], *refs),
+            out_shape=piece[n],
             in_specs=[HBM],
             out_specs=VMEM,
             scratch_shapes=[pltpu.SemaphoreType.DMA],
             compiler_params=params(4),
-            cost_estimate=cost(0, 2 * piece.size),
+            cost_estimate=cost(0, 2 * piece[n].size),
         )(out_weight)
+
+    def attend(slots, n):
+        return pl.pallas_call(
+            lambda *refs: attend_kernel(slots, bounds[n], beams, heads, kv_count, per_kv, tokens, *refs),
+            out_shape=[jax.ShapeDtypeStruct((count + 16, HD), BF)] * len(slots) + [piece[n]],
+            in_specs=[HBM] * 3 + [VMEM] * (len(slots) + 2),
+            out_specs=[VMEM] * (len(slots) + 1),
+            scratch_shapes=[pltpu.SMEM(lengths.shape, jnp.int32)] * 2 + [pltpu.SemaphoreType.DMA((3,))],
+            compiler_params=params(12),
+            cost_estimate=cost(4 * count * len(slots) * tokens * HD, 2 * piece[n].size),
+        )(lengths, parents, out_weight, kt, vt, *[stacks[k] for k in slots])
 
     packet = pl.pallas_call(
         lambda *refs: pack_kernel(heads, kv_count, *refs),
@@ -245,21 +276,10 @@
     vt = jnp.transpose(cache_values[0], (1, 0, 2))
     stack = jnp.stack([packet] + partners(packet, "beam"))
     stacks = [stack] + partners(stack, "ctx")
-    first_piece = fetch(0)
-
-    state = jax.ShapeDtypeStruct((count + 16, HD), BF)
-    *states, second_piece = pl.pallas_call(
-        lambda *refs: attend_kernel(ctx_count, beams, heads, kv_count, per_kv, tokens, *refs),
-        out_shape=[state] * ctx_count + [piece],
-        in_specs=[HBM] * 3 + [VMEM] * (ctx_count + 2),
-        out_specs=[VMEM] * (ctx_count + 1),
-        scratch_shapes=[pltpu.SMEM(lengths.shape, jnp.int32)] * 2 + [pltpu.SemaphoreType.DMA((3,))],
-        compiler_params=params(8),
-        cost_estimate=cost(4 * beams * H * tokens * HD, 2 * piece.size),
-        name="attend",
-    )(lengths, parents, out_weight, kt, vt, *stacks)
-    states = [states[0]] + partners(states, "ctx")
-    third_piece = fetch(2)
+    own_state, piece0 = attend((0,), 0)
+    *states, piece1 = attend(tuple(range(1, ctx_count)), 1)
+    states = [own_state] + partners([None] + states, "ctx")
+    piece2 = fetch(2)
 
     attended = pl.pallas_call(
         lambda *refs: merge_kernel(ctx_count, beams, heads, kv_count, per_kv, *refs),
@@ -271,25 +291,33 @@
     )(stack, *states)
     rows_of = [attended] + partners(attended, "beam")
 
+    piece3 = fetch(3)
+
     columns = out_weight.shape[1] // ctx_count
-    parts = pl.pallas_call(
-        lambda *refs: project_kernel(ctx_count, beams, heads, *refs),
-        out_shape=[jax.ShapeDtypeStruct((beams, columns), F32)] * ctx_count,
-        in_specs=[VMEM] * (beams + PIECES - 1) + [HBM],
-        out_specs=[VMEM] * ctx_count,
-        scratch_shapes=[
-            pltpu.VMEM(piece.shape, BF),
-            pltpu.VMEM((8 * heads, HD), F32),
-            pltpu.VMEM((8, heads * HD), BF),
-            pltpu.SemaphoreType.DMA,
-        ],
-        compiler_params=params(16),
-        cost_estimate=cost(16 * out_weight.size, 2 * piece.size),
+    part = jax.ShapeDtypeStruct((beams, columns), F32)
+    wide = jax.ShapeDtypeStruct((8, heads * HD), BF)
+    *parts, piece4, wide = pl.pallas_call(
+        lambda *refs: project_kernel(ctx_count, beams, heads, bounds, *refs),
+        out_shape=[part] * (ctx_count - 1) + [piece[4], wide],
+        in_specs=[VMEM] * (beams + 4) + [HBM],
+        out_specs=[VMEM] * (ctx_count + 1),
+        scratch_shapes=[pltpu.VMEM((8 * heads, HD), F32), pltpu.SemaphoreType.DMA],
+        compiler_params=params(8),
+        cost_estimate=cost(12 * out_weight.size, 2 * piece[4].size),
         name="project",
-    )(*rows_of, first_piece, second_piece, third_piece, out_weight)
-    total = parts[0]
-    for part in partners(parts, "ctx"):
-        total = total + part
+    )(*rows_of, piece0, piece1, piece2, piece3, out_weight)
+    others = partners([None] + parts, "ctx")
+    total = pl.pallas_call(
+        lambda *refs: home_kernel(ctx_count, beams, bounds, *refs),
+        out_shape=part,
+        in_specs=[VMEM] * 6,
+        out_specs=VMEM,
+        compiler_params=params(4),
+        cost_estimate=cost(4 * out_weight.size, 0),
+        name="home",
+    )(wide, piece0, piece1, piece2, piece3, piece4)
+    for other in others:
+        total = total + other
     return total.astype(BF)
 
 

time: 47.8 us -> 45.4 us (0.950)
  waiting for transfers between devices: 10.4 us -> 6.94 us
  Pallas kernels: 18.4 us -> 19.4 us
    ppermute x15, waiting for transfers between devices: 10.4 us -> 6.94 us  [partners(): found.append(lax.ppermute(array, axis, [(i, i ^ k) for i in range(length)]))]
    pallas_call x4 -> x6, Pallas kernels: 17.2 us -> 18.3 us  [the longest x2 6.19 us: fetch(): pl.pallas_call(lambda *refs: fetch_kernel(bounds[n], *refs), out_shape=pi...]
  transfers between devices with their start and end apart: 15 -> 15, of which waited for: 8 -> 7; matrix products, arithmetic and copies ran while one was open for 4% -> 4% of each run, Pallas kernels for 14% -> 21%
where the time goes in v3:
time: 45.4 us; the launch traced here: 45.1 us
  Pallas kernels  19.4 us (43%)
  starting transfers between devices  16 us (35%)
  waiting for transfers between devices  6.94 us (15%)
  local copies, waits for them, and re-layouts  1.92 us (4%)
  other arithmetic  0.62 us (1%)
    ppermute x15, starting transfers between devices, partners(): found.append(lax.ppermute(array, axis, [(i, i ^ k) for i in range(length)]))  16 us
    ppermute x15, waiting for transfers between devices, partners(): found.append(lax.ppermute(array, axis, [(i, i ^ k) for i in range(length)]))  6.94 us
    pallas_call x2, Pallas kernels, fetch(): pl.pallas_call(lambda *refs: fetch_kernel(bounds[n], *refs), out_shape=pi...  6.19 us
    pallas_call x2, Pallas kernels, attend(): pl.pallas_call(lambda *refs: attend_kernel(slots, bounds[n], beams, heads...  5.91 us
    pallas_call x1, Pallas kernels, step(): pl.pallas_call(lambda *refs: project_kernel(ctx_count, beams, heads, boun...  4.99 us
    transpose x1, local copies, waits for them, and re-layouts, step(): vt = jnp.transpose(cache_values[0], (1, 0, 2))  1.92 us
    pallas_call x1, Pallas kernels, step(): pl.pallas_call(lambda *refs: home_kernel(ctx_count, beams, bounds, *refs)...  1.19 us
  transfers between devices with their start and end apart: 15, of which 7 were waited for; matrix products, arithmetic and copies ran while one was open for 4% of the time, Pallas kernels for 21%

profile of v3, /device:TPU:0, one launch (start us, length us, event | category | flops | bytes accessed | tf_op | source)
XLA Modules:
  0.0 45.1 jit_solution(5823191127302377862)
XLA Ops:
  0.0 0.8 %pack.1 = bf16[48,128]{1,0:T(8,128)(2,1)S(1)} custom-call(bf16[1,4096]{1,0:T(2,128)(2,1)} %refs_0_.5, bf16[1,1024]{1,0:T(2,128)(2,1)} %refs_1_.3, bf16[1,1024]{1,0:T(2,128)(2,1)} %refs_2_.3), custom_call_target="tpu_custom_call" | custom-call | tf_op jit(solution)/shard_map/pack/pallas_call | solution.py:265
  0.8 5.1 %collective-permute-start.2 = (bf16[48,128]{1,0:T(8,128)(2,1)S(1)}, bf16[48,128]{1,0:T(8,128)(2,1)S(1)}, u32[]{:S(2)}, u32[]{:S(2)}) collective-permute-start(bf16[48,128]{1,0:T(8,128)(2,1)S(1)} %pack.1), channel_id=1, source_target_pairs={{0,12},{4,8},{8,4},{12,0},{1,13},{5,9},{9,5},{13,1},{2,14},{6,10},... | collective-permute-start | bytes 36872 | tf_op jit(solution)/shard_map/ppermute | solution.py:40
  5.9 0.6 %collective-permute-start = (bf16[48,128]{1,0:T(8,128)(2,1)S(1)}, bf16[48,128]{1,0:T(8,128)(2,1)S(1)}, u32[]{:S(2)}, u32[]{:S(2)}) collective-permute-start(bf16[48,128]{1,0:T(8,128)(2,1)S(1)} %pack.1), channel_id=1, source_target_pairs={{0,4},{4,0},{8,12},{12,8},{1,5},{5,1},{9,13},{13,9},{2,6},{6,2},{1... | collective-permute-start | bytes 36872 | tf_op jit(solution)/shard_map/ppermute | solution.py:40
  6.6 1.0 %collective-permute-done.2 = bf16[48,128]{1,0:T(8,128)(2,1)S(1)} collective-permute-done((bf16[48,128]{1,0:T(8,128)(2,1)S(1)}, bf16[48,128]{1,0:T(8,128)(2,1)S(1)}, u32[]{:S(2)}, u32[]{:S(2)}) %collective-permute-start.2) | collective-permute-done | bytes 12320 | tf_op jit(solution)/shard_map/ppermute | solution.py:40
  7.6 2.9 %collective-permute-done.1 = bf16[48,128]{1,0:T(8,128)(2,1)S(1)} collective-permute-done((bf16[48,128]{1,0:T(8,128)(2,1)S(1)}, bf16[48,128]{1,0:T(8,128)(2,1)S(1)}, u32[]{:S(2)}, u32[]{:S(2)}) %collective-permute-start.1) | collective-permute-done | bytes 12320 | tf_op jit(solution)/shard_map/ppermute | solution.py:40
  10.5 0.1 collective-permute-start.5
  10.6 1.6 %collective-permute-start.4 = (bf16[4,48,128]{2,1,0:T(8,128)(2,1)S(1)}, bf16[4,48,128]{2,1,0:T(8,128)(2,1)S(1)}, u32[]{:S(2)}, u32[]{:S(2)}) collective-permute-start(bf16[4,48,128]{2,1,0:T(8,128)(2,1)S(1)} %pad_maximum_fusion.refs_5_.refs_0_), channel_id=1, source_target_pairs={{0,2},{1,3},{2,0},{3,1},{4,6},{5,7},{6,4},{7,5},{8,10},{9,11},{10,... | collective-permute-start | bytes 147464 | tf_op jit(solution)/shard_map/ppermute | solution.py:40
  12.2 0.3 collective-permute-start.3
  12.5 1.9 %copy_bitcast_fusion = (bf16[8,512,128]{2,1,0:T(8,128)(2,1)S(1)}, bf16[8,512,128]{2,1,0:T(8,128)(2,1)S(1)}) fusion(bf16[1,512,8,128]{3,2,1,0:T(8,128)(2,1)} %param.12, bf16[1,512,8,128]{3,2,1,0:T(8,128)(2,1)} %param.11), kind=kLoop, calls=%fused_computation | loop fusion | bytes 4194304 | tf_op jit(solution)/shard_map/transpose | solution.py:276
  14.4 0.2 collective-permute-done.5.refs_7_
  14.6 0.9 %collective-permute-done.4.refs_6_ = bf16[4,48,128]{2,1,0:T(8,128)(2,1)S(1)} collective-permute-done((bf16[4,48,128]{2,1,0:T(8,128)(2,1)S(1)}, bf16[4,48,128]{2,1,0:T(8,128)(2,1)S(1)}, u32[]{:S(2)}, u32[]{:S(2)}) %collective-permute-start.4) | collective-permute-done | bytes 49184 | tf_op jit(solution)/shard_map/ppermute | solution.py:40
  15.5 3.7 %shard_map.83 = (bf16[144,128]{1,0:T(8,128)(2,1)S(1)}, bf16[144,128]{1,0:T(8,128)(2,1)S(1)}, bf16[144,128]{1,0:T(8,128)(2,1)S(1)}, bf16[1024,4096]{1,0:T(8,128)(2,1)S(1)}) custom-call(s32[4]{0:T(128)} %refs_0_.7, s32[4]{0:T(128)} %refs_1_.5, bf16[4096,4096]{1,0:T(8,128)(2,1)} %refs_8_.1, bf16[8,512,128]{2,1,0:T(8,128)(2,1)S(1)} %get-tuple-element.28.refs_3_, ...), custom_call_target="tpu_custom_call" | custom-call | flops 100663296 | bytes 8388608 | tf_op jit(solution)/shard_map/pallas_call | solution.py:255
  19.2 0.2 collective-permute-start.6
  19.4 1.1 %collective-permute-start.7 = (bf16[144,128]{1,0:T(8,128)(2,1)S(1)}, bf16[144,128]{1,0:T(8,128)(2,1)S(1)}, u32[]{:S(2)}, u32[]{:S(2)}) collective-permute-start(bf16[144,128]{1,0:T(8,128)(2,1)S(1)} %get-tuple-element.18), channel_id=1, source_target_pairs={{0,2},{1,3},{2,0},{3,1},{4,6},{5,7},{6,4},{7,5},{8,10},{9,11},{10,... | collective-permute-start | bytes 110600 | tf_op jit(solution)/shard_map/ppermute | solution.py:40
  20.5 0.6 %collective-permute-start.8 = (bf16[144,128]{1,0:T(8,128)(2,1)S(1)}, bf16[144,128]{1,0:T(8,128)(2,1)S(1)}, u32[]{:S(2)}, u32[]{:S(2)}) collective-permute-start(bf16[144,128]{1,0:T(8,128)(2,1)S(1)} %get-tuple-element.19), channel_id=1, source_target_pairs={{0,3},{1,2},{2,1},{3,0},{4,7},{5,6},{6,5},{7,4},{8,11},{9,10},{10,... | collective-permute-start | bytes 110600 | tf_op jit(solution)/shard_map/ppermute | solution.py:40
  21.1 2.3 %shard_map.82 = (bf16[144,128]{1,0:T(8,128)(2,1)S(1)}, bf16[512,4096]{1,0:T(8,128)(2,1)S(1)}) custom-call(s32[4]{0:T(128)} %refs_0_.7, s32[4]{0:T(128)} %refs_1_.5, bf16[4096,4096]{1,0:T(8,128)(2,1)} %refs_8_.1, bf16[8,512,128]{2,1,0:T(8,128)(2,1)S(1)} %get-tuple-element.28.refs_3_, bf16[8,512,128]{2,1,0:T(8,128)(2,1)S(1)} %get-tuple-element.27.refs_4_, ...), custom_call_target="tpu_custom_call" | custom-call | flops 33554432 | bytes 4194304 | tf_op jit(solution)/shard_map/pallas_call | solution.py:255
  23.4 0.0 collective-permute-done.6.refs_2_
  23.4 0.6 %collective-permute-done.8.refs_4_ = bf16[144,128]{1,0:T(8,128)(2,1)S(1)} collective-permute-done((bf16[144,128]{1,0:T(8,128)(2,1)S(1)}, bf16[144,128]{1,0:T(8,128)(2,1)S(1)}, u32[]{:S(2)}, u32[]{:S(2)}) %collective-permute-start.8) | collective-permute-done | bytes 36896 | tf_op jit(solution)/shard_map/ppermute | solution.py:40
  23.9 0.4 merge.1.refs_0_
  24.4 1.5 %collective-permute-start.11 = (bf16[4,32,128]{2,1,0:T(8,128)(2,1)S(1)}, bf16[4,32,128]{2,1,0:T(8,128)(2,1)S(1)}, u32[]{:S(2)}, u32[]{:S(2)}) collective-permute-start(bf16[4,32,128]{2,1,0:T(8,128)(2,1)S(1)} %merge.1.refs_0_), channel_id=1, source_target_pairs={{0,12},{4,8},{8,4},{12,0},{1,13},{5,9},{9,5},{13,1},{2,14},{6,10},... | collective-permute-start | bytes 98312 | tf_op jit(solution)/shard_map/ppermute | solution.py:40
  25.9 0.6 %collective-permute-start.10 = (bf16[4,32,128]{2,1,0:T(8,128)(2,1)S(1)}, bf16[4,32,128]{2,1,0:T(8,128)(2,1)S(1)}, u32[]{:S(2)}, u32[]{:S(2)}) collective-permute-start(bf16[4,32,128]{2,1,0:T(8,128)(2,1)S(1)} %merge.1.refs_0_), channel_id=1, source_target_pairs={{0,8},{4,12},{8,0},{12,4},{1,9},{5,13},{9,1},{13,5},{2,10},{6,14},... | collective-permute-start | bytes 98312 | tf_op jit(solution)/shard_map/ppermute | solution.py:40
  26.5 2.3 %collective-permute-start.9 = (bf16[4,32,128]{2,1,0:T(8,128)(2,1)S(1)}, bf16[4,32,128]{2,1,0:T(8,128)(2,1)S(1)}, u32[]{:S(2)}, u32[]{:S(2)}) collective-permute-start(bf16[4,32,128]{2,1,0:T(8,128)(2,1)S(1)} %merge.1.refs_0_), channel_id=1, source_target_pairs={{0,4},{4,0},{8,12},{12,8},{1,5},{5,1},{9,13},{13,9},{2,6},{6,2},{1... | collective-permute-start | bytes 98312 | tf_op jit(solution)/shard_map/ppermute | solution.py:40
  28.8 2.2 %shard_map.84.refs_6_.refs_3_ = bf16[512,4096]{1,0:T(8,128)(2,1)S(1)} custom-call(bf16[4096,4096]{1,0:T(8,128)(2,1)} %refs_8_.1), custom_call_target="tpu_custom_call" | custom-call | bytes 4194304 | tf_op jit(solution)/shard_map/pallas_call | solution.py:244
  31.0 4.0 %shard_map.85.refs_7_.refs_4_ = bf16[1280,4096]{1,0:T(8,128)(2,1)S(1)} custom-call(bf16[4096,4096]{1,0:T(8,128)(2,1)} %refs_8_.1), custom_call_target="tpu_custom_call" | custom-call | bytes 10485760 | tf_op jit(solution)/shard_map/pallas_call | solution.py:244
  35.0 5.0 %project.1 = (f32[4,1024]{1,0:T(4,128)S(1)}, f32[4,1024]{1,0:T(4,128)S(1)}, f32[4,1024]{1,0:T(4,128)S(1)}, bf16[768,4096]{1,0:T(8,128)(2,1)S(1)}, bf16[8,4096]{1,0:T(8,128)(2,1)S(1)}) custom-call(bf16[4,32,128]{2,1,0:T(8,128)(2,1)S(1)} %merge.1.refs_0_, bf16[4,32,128]{2,1,0:T(8,128)(2,1)S(1)} %collective-permute-done.9.refs_1_, ...), custom_call_target="tpu_custom_call" | custom-call | flops 201326592 | bytes 6291456 | tf_op jit(solution)/shard_map/project/pallas_call | solution.py:299
  40.0 0.1 collective-permute-start.12
  40.1 1.2 %collective-permute-start.13 = (f32[4,1024]{1,0:T(4,128)S(1)}, f32[4,1024]{1,0:T(4,128)S(1)}, u32[]{:S(2)}, u32[]{:S(2)}) collective-permute-start(f32[4,1024]{1,0:T(4,128)S(1)} %get-tuple-element.25), channel_id=1, source_target_pairs={{0,2},{1,3},{2,0},{3,1},{4,6},{5,7},{6,4},{7,5},{8,10},{9,11},{10,... | collective-permute-start | bytes 49160 | tf_op jit(solution)/shard_map/ppermute | solution.py:40
  41.3 0.7 %collective-permute-start.14 = (f32[4,1024]{1,0:T(4,128)S(1)}, f32[4,1024]{1,0:T(4,128)S(1)}, u32[]{:S(2)}, u32[]{:S(2)}) collective-permute-start(f32[4,1024]{1,0:T(4,128)S(1)} %get-tuple-element.26), channel_id=1, source_target_pairs={{0,3},{1,2},{2,1},{3,0},{4,7},{5,6},{6,5},{7,4},{8,11},{9,10},{10,... | collective-permute-start | bytes 49160 | tf_op jit(solution)/shard_map/ppermute | solution.py:40
  42.0 1.2 %home.1 = f32[4,1024]{1,0:T(4,128)S(1)} custom-call(bf16[8,4096]{1,0:T(8,128)(2,1)S(1)} %get-tuple-element.22.refs_0_, bf16[512,4096]{1,0:T(8,128)(2,1)S(1)} %get-tuple-element.20.refs_4_.refs_1_, bf16[1024,4096]{1,0:T(8,128)(2,1)S(1)} %get-tuple-element.21.refs_5_.refs_2_, bf16[512,4096]{1,0:T(8,128)(2,1)S(1)} %shard_map.84.refs_6_.refs_3_, ...), custom_call_target="tpu_custom_call" | custom-call | flops 67108864 | tf_op jit(solution)/shard_map/home/pallas_call | solution.py:310
  43.2 0.8 %collective-permute-done.13 = f32[4,1024]{1,0:T(4,128)S(1)} collective-permute-done((f32[4,1024]{1,0:T(4,128)S(1)}, f32[4,1024]{1,0:T(4,128)S(1)}, u32[]{:S(2)}, u32[]{:S(2)}) %collective-permute-start.13) | collective-permute-done | bytes 16416 | tf_op jit(solution)/shard_map/ppermute | solution.py:40
  43.9 0.5 %collective-permute-done.14 = f32[4,1024]{1,0:T(4,128)S(1)} collective-permute-done((f32[4,1024]{1,0:T(4,128)S(1)}, f32[4,1024]{1,0:T(4,128)S(1)}, u32[]{:S(2)}, u32[]{:S(2)}) %collective-permute-start.14) | collective-permute-done | bytes 16416 | tf_op jit(solution)/shard_map/ppermute | solution.py:40
  44.5 0.6 %add_convert_fusion = bf16[4,1024]{1,0:T(4,128)(2,1)} fusion(f32[4,1024]{1,0:T(4,128)S(1)} %collective-permute-done.14, f32[4,1024]{1,0:T(4,128)S(1)} %collective-permute-done.13, f32[4,1024]{1,0:T(4,128)S(1)} %home.1, f32[4,1024]{1,0:T(4,128)S(1)} %collective-permute-done.12), kind=kLoop, calls=%fused_computation.3 | loop fusion | flops 16384 | bytes 73728 | tf_op jit(solution)/shard_map/convert_element_type | solution.py:321
  (9 shorter events, 0.0 us)
Async XLA Ops:
  0.8 6.8 %collective-permute-start.2 = (bf16[48,128]{1,0:T(8,128)(2,1)S(1)}, bf16[48,128]{1,0:T(8,128)(2,1)S(1)}, u32[]{:S(2)}, u32[]{:S(2)}) collective-permute-start(bf16[48,128]{1,0:T(8,128)(2,1)S(1)} %pack.1), channel_id=1, source_target_pairs={{0,12},{4,8},{8,4},{12,0},{1,13},{5,9},{9,5},{13,1},{2,14},{6,10},... | collective-permute-start | bytes 36872 | tf_op jit(solution)/shard_map/ppermute | solution.py:40
  5.9 4.6 %collective-permute-start.1 = (bf16[48,128]{1,0:T(8,128)(2,1)S(1)}, bf16[48,128]{1,0:T(8,128)(2,1)S(1)}, u32[]{:S(2)}, u32[]{:S(2)}) collective-permute-start(bf16[48,128]{1,0:T(8,128)(2,1)S(1)} %pack.1), channel_id=1, source_target_pairs={{0,8},{4,12},{8,0},{12,4},{1,9},{5,13},{9,1},{13,5},{2,10},{6,14},... | collective-permute-start | bytes 36872 | tf_op jit(solution)/shard_map/ppermute | solution.py:40
  5.9 4.6 %collective-permute-start = (bf16[48,128]{1,0:T(8,128)(2,1)S(1)}, bf16[48,128]{1,0:T(8,128)(2,1)S(1)}, u32[]{:S(2)}, u32[]{:S(2)}) collective-permute-start(bf16[48,128]{1,0:T(8,128)(2,1)S(1)} %pack.1), channel_id=1, source_target_pairs={{0,4},{4,0},{8,12},{12,8},{1,5},{5,1},{9,13},{13,9},{2,6},{6,2},{1... | collective-permute-start | bytes 36872 | tf_op jit(solution)/shard_map/ppermute | solution.py:40
  10.5 4.0 %collective-permute-start.5 = (bf16[4,48,128]{2,1,0:T(8,128)(2,1)S(1)}, bf16[4,48,128]{2,1,0:T(8,128)(2,1)S(1)}, u32[]{:S(2)}, u32[]{:S(2)}) collective-permute-start(bf16[4,48,128]{2,1,0:T(8,128)(2,1)S(1)} %pad_maximum_fusion.refs_5_.refs_0_), channel_id=1, source_target_pairs={{0,3},{1,2},{2,1},{3,0},{4,7},{5,6},{6,5},{7,4},{8,11},{9,10},{10,... | collective-permute-start | bytes 147464 | tf_op jit(solution)/shard_map/ppermute | solution.py:40
  10.6 4.9 %collective-permute-start.4 = (bf16[4,48,128]{2,1,0:T(8,128)(2,1)S(1)}, bf16[4,48,128]{2,1,0:T(8,128)(2,1)S(1)}, u32[]{:S(2)}, u32[]{:S(2)}) collective-permute-start(bf16[4,48,128]{2,1,0:T(8,128)(2,1)S(1)} %pad_maximum_fusion.refs_5_.refs_0_), channel_id=1, source_target_pairs={{0,2},{1,3},{2,0},{3,1},{4,6},{5,7},{6,4},{7,5},{8,10},{9,11},{10,... | collective-permute-start | bytes 147464 | tf_op jit(solution)/shard_map/ppermute | solution.py:40
  12.2 3.3 %collective-permute-start.3 = (bf16[4,48,128]{2,1,0:T(8,128)(2,1)S(1)}, bf16[4,48,128]{2,1,0:T(8,128)(2,1)S(1)}, u32[]{:S(2)}, u32[]{:S(2)}) collective-permute-start(bf16[4,48,128]{2,1,0:T(8,128)(2,1)S(1)} %pad_maximum_fusion.refs_5_.refs_0_), channel_id=1, source_target_pairs={{0,1},{1,0},{2,3},{3,2},{4,5},{5,4},{6,7},{7,6},{8,9},{9,8},{10,11... | collective-permute-start | bytes 147464 | tf_op jit(solution)/shard_map/ppermute | solution.py:40
  19.2 4.2 %collective-permute-start.6 = (bf16[144,128]{1,0:T(8,128)(2,1)S(1)}, bf16[144,128]{1,0:T(8,128)(2,1)S(1)}, u32[]{:S(2)}, u32[]{:S(2)}) collective-permute-start(bf16[144,128]{1,0:T(8,128)(2,1)S(1)} %get-tuple-element.17), channel_id=1, source_target_pairs={{0,1},{1,0},{2,3},{3,2},{4,5},{5,4},{6,7},{7,6},{8,9},{9,8},{10,11... | collective-permute-start | bytes 110600 | tf_op jit(solution)/shard_map/ppermute | solution.py:40
  19.4 4.0 %collective-permute-start.7 = (bf16[144,128]{1,0:T(8,128)(2,1)S(1)}, bf16[144,128]{1,0:T(8,128)(2,1)S(1)}, u32[]{:S(2)}, u32[]{:S(2)}) collective-permute-start(bf16[144,128]{1,0:T(8,128)(2,1)S(1)} %get-tuple-element.18), channel_id=1, source_target_pairs={{0,2},{1,3},{2,0},{3,1},{4,6},{5,7},{6,4},{7,5},{8,10},{9,11},{10,... | collective-permute-start | bytes 110600 | tf_op jit(solution)/shard_map/ppermute | solution.py:40
  20.5 3.4 %collective-permute-start.8 = (bf16[144,128]{1,0:T(8,128)(2,1)S(1)}, bf16[144,128]{1,0:T(8,128)(2,1)S(1)}, u32[]{:S(2)}, u32[]{:S(2)}) collective-permute-start(bf16[144,128]{1,0:T(8,128)(2,1)S(1)} %get-tuple-element.19), channel_id=1, source_target_pairs={{0,3},{1,2},{2,1},{3,0},{4,7},{5,6},{6,5},{7,4},{8,11},{9,10},{10,... | collective-permute-start | bytes 110600 | tf_op jit(solution)/shard_map/ppermute | solution.py:40
  24.4 10.7 %collective-permute-start.11 = (bf16[4,32,128]{2,1,0:T(8,128)(2,1)S(1)}, bf16[4,32,128]{2,1,0:T(8,128)(2,1)S(1)}, u32[]{:S(2)}, u32[]{:S(2)}) collective-permute-start(bf16[4,32,128]{2,1,0:T(8,128)(2,1)S(1)} %merge.1.refs_0_), channel_id=1, source_target_pairs={{0,12},{4,8},{8,4},{12,0},{1,13},{5,9},{9,5},{13,1},{2,14},{6,10},... | collective-permute-start | bytes 98312 | tf_op jit(solution)/shard_map/ppermute | solution.py:40
  25.9 9.1 %collective-permute-start.10 = (bf16[4,32,128]{2,1,0:T(8,128)(2,1)S(1)}, bf16[4,32,128]{2,1,0:T(8,128)(2,1)S(1)}, u32[]{:S(2)}, u32[]{:S(2)}) collective-permute-start(bf16[4,32,128]{2,1,0:T(8,128)(2,1)S(1)} %merge.1.refs_0_), channel_id=1, source_target_pairs={{0,8},{4,12},{8,0},{12,4},{1,9},{5,13},{9,1},{13,5},{2,10},{6,14},... | collective-permute-start | bytes 98312 | tf_op jit(solution)/shard_map/ppermute | solution.py:40
  26.5 8.5 %collective-permute-start.9 = (bf16[4,32,128]{2,1,0:T(8,128)(2,1)S(1)}, bf16[4,32,128]{2,1,0:T(8,128)(2,1)S(1)}, u32[]{:S(2)}, u32[]{:S(2)}) collective-permute-start(bf16[4,32,128]{2,1,0:T(8,128)(2,1)S(1)} %merge.1.refs_0_), channel_id=1, source_target_pairs={{0,4},{4,0},{8,12},{12,8},{1,5},{5,1},{9,13},{13,9},{2,6},{6,2},{1... | collective-permute-start | bytes 98312 | tf_op jit(solution)/shard_map/ppermute | solution.py:40
  40.0 3.1 %collective-permute-start.12 = (f32[4,1024]{1,0:T(4,128)S(1)}, f32[4,1024]{1,0:T(4,128)S(1)}, u32[]{:S(2)}, u32[]{:S(2)}) collective-permute-start(f32[4,1024]{1,0:T(4,128)S(1)} %get-tuple-element.24), channel_id=1, source_target_pairs={{0,1},{1,0},{2,3},{3,2},{4,5},{5,4},{6,7},{7,6},{8,9},{9,8},{10,11... | collective-permute-start | bytes 49160 | tf_op jit(solution)/shard_map/ppermute | solution.py:40
  40.1 3.8 %collective-permute-start.13 = (f32[4,1024]{1,0:T(4,128)S(1)}, f32[4,1024]{1,0:T(4,128)S(1)}, u32[]{:S(2)}, u32[]{:S(2)}) collective-permute-start(f32[4,1024]{1,0:T(4,128)S(1)} %get-tuple-element.25), channel_id=1, source_target_pairs={{0,2},{1,3},{2,0},{3,1},{4,6},{5,7},{6,4},{7,5},{8,10},{9,11},{10,... | collective-permute-start | bytes 49160 | tf_op jit(solution)/shard_map/ppermute | solution.py:40
  41.3 3.2 %collective-permute-start.14 = (f32[4,1024]{1,0:T(4,128)S(1)}, f32[4,1024]{1,0:T(4,128)S(1)}, u32[]{:S(2)}, u32[]{:S(2)}) collective-permute-start(f32[4,1024]{1,0:T(4,128)S(1)} %get-tuple-element.26), channel_id=1, source_target_pairs={{0,3},{1,2},{2,1},{3,0},{4,7},{5,6},{6,5},{7,4},{8,11},{9,10},{10,... | collective-permute-start | bytes 49160 | tf_op jit(solution)/shard_map/ppermute | solution.py:40

commit v4 on v3

--- a/solution.py
+++ b/solution.py
@@ -21,7 +21,7 @@
 F32 = jnp.float32
 VMEM = pl.BlockSpec(memory_space=pltpu.VMEM)
 HBM = pl.BlockSpec(memory_space=pltpu.HBM)
-SHARES = (4, 8, 4, 10, 6)
+SHARES = (5, 5, 5, 10, 7)
 
 
 def params(mib):
@@ -32,13 +32,13 @@
     return pl.CostEstimate(flops=flops, bytes_accessed=moved, transcendentals=0)
 
 
+def partner(array, axis, k):
+    return lax.ppermute(array, axis, [(i, i ^ k) for i in range(lax.axis_size(axis))])
+
+
 def partners(arrays, axis):
-    length = lax.axis_size(axis)
-    found = []
-    for k in range(1, length):
-        array = arrays[k] if isinstance(arrays, (list, tuple)) else arrays
-        found.append(lax.ppermute(array, axis, [(i, i ^ k) for i in range(length)]))
-    return found
+    each = isinstance(arrays, (list, tuple))
+    return [partner(arrays[k] if each else arrays, axis, k) for k in range(1, lax.axis_size(axis))]
 
 
 def pack_kernel(heads, kv_count, q_hbm, k_hbm, v_hbm, out_ref, q_ref, k_ref, v_ref, rows, sems):
@@ -188,7 +188,7 @@
     )[:beams]
 
 
-def project_kernel(ctx_count, beams, heads, bounds, *refs):
+def project_kernel(ctx_count, far, beams, heads, bounds, *refs):
     rows_of, pieces, w_hbm = refs[:beams], refs[beams : beams + 4], refs[beams + 4]
     outs, (last, wide), (laid, sem) = refs[beams + 5 : -4], refs[-4:-2], refs[-2:]
     copy = pltpu.make_async_copy(w_hbm.at[pl.ds(bounds[4], last.shape[0])], last, sem)
@@ -204,22 +204,22 @@
         wide[:, h * HD : (h + 1) * HD] = laid[pl.ds(h, 8, stride=heads), :].astype(BF)
     columns = last.shape[1] // ctx_count
     width = min(512, columns)
-    places = [(k, j) for k in range(1, ctx_count) for j in range(0, columns, width)]
-    for k, j in places:
+    places = [(n, k, j) for n, k in enumerate(far) for j in range(0, columns, width)]
+    for n, k, j in places:
         at = pl.multiple_of((c ^ k) * columns + j, 128)
-        outs[k - 1][:, j : j + width] = chunk(wide, pieces, bounds[:5], beams, at, width)
+        outs[n][:, j : j + width] = chunk(wide, pieces, bounds[:5], beams, at, width)
     copy.wait()
-    for k, j in places:
+    for n, k, j in places:
         at = pl.multiple_of((c ^ k) * columns + j, 128)
-        outs[k - 1][:, j : j + width] += chunk(wide, [last], bounds[4:], beams, at, width)
-
-
-def home_kernel(ctx_count, beams, bounds, wide, *refs):
+        outs[n][:, j : j + width] += chunk(wide, [last], bounds[4:], beams, at, width)
+
+
+def near_kernel(ctx_count, k, beams, bounds, wide, *refs):
     pieces, out_ref = refs[:-1], refs[-1]
     columns = pieces[0].shape[1] // ctx_count
     width = min(512, columns)
     for j in range(0, columns, width):
-        at = pl.multiple_of(lax.axis_index("ctx") * columns + j, 128)
+        at = pl.multiple_of((lax.axis_index("ctx") ^ k) * columns + j, 128)
         out_ref[:, j : j + width] = chunk(wide, pieces, bounds, beams, at, width)
 
 
@@ -296,26 +296,32 @@
     columns = out_weight.shape[1] // ctx_count
     part = jax.ShapeDtypeStruct((beams, columns), F32)
     wide = jax.ShapeDtypeStruct((8, heads * HD), BF)
+    far = tuple(range(2, ctx_count))
     *parts, piece4, wide = pl.pallas_call(
-        lambda *refs: project_kernel(ctx_count, beams, heads, bounds, *refs),
-        out_shape=[part] * (ctx_count - 1) + [piece[4], wide],
+        lambda *refs: project_kernel(ctx_count, far, beams, heads, bounds, *refs),
+        out_shape=[part] * len(far) + [piece[4], wide],
         in_specs=[VMEM] * (beams + 4) + [HBM],
-        out_specs=[VMEM] * (ctx_count + 1),
+        out_specs=[VMEM] * (len(far) + 2),
         scratch_shapes=[pltpu.VMEM((8 * heads, HD), F32), pltpu.SemaphoreType.DMA],
         compiler_params=params(8),
-        cost_estimate=cost(12 * out_weight.size, 2 * piece[4].size),
+        cost_estimate=cost(8 * out_weight.size, 2 * piece[4].size),
         name="project",
     )(*rows_of, piece0, piece1, piece2, piece3, out_weight)
-    others = partners([None] + parts, "ctx")
-    total = pl.pallas_call(
-        lambda *refs: home_kernel(ctx_count, beams, bounds, *refs),
-        out_shape=part,
-        in_specs=[VMEM] * 6,
-        out_specs=VMEM,
-        compiler_params=params(4),
-        cost_estimate=cost(4 * out_weight.size, 0),
-        name="home",
-    )(wide, piece0, piece1, piece2, piece3, piece4)
+
+    def near(k):
+        return pl.pallas_call(
+            lambda *refs: near_kernel(ctx_count, k, beams, bounds, *refs),
+            out_shape=part,
+            in_specs=[VMEM] * 6,
+            out_specs=VMEM,
+            compiler_params=params(4),
+            cost_estimate=cost(4 * out_weight.size, 0),
+        )(wide, piece0, piece1, piece2, piece3, piece4)
+
+    others = [partner(part, "ctx", k) for k, part in zip(far, parts)]
+    core = near(1)
+    others.append(partner(core, "ctx", 1))
+    total = near(0)
     for other in others:
         total = total + other
     return total.astype(BF)

time: 45.4 us -> 45.6 us (level)
  Pallas kernels: 19.4 us -> 20.1 us
    pallas_call x2 -> x3, Pallas kernels: 6.18 us -> 7.09 us  [the longest x1 4.71 us: step(): pl.pallas_call(lambda *refs: project_kernel(ctx_count, far, beams, heads,...]
    pallas_call x2, Pallas kernels: 5.91 us -> 5.31 us  [attend(): pl.pallas_call(lambda *refs: attend_kernel(slots, bounds[n], beams, heads...]
  transfers between devices with their start and end apart: 15 -> 15, of which waited for: 7 -> 7; matrix products, arithmetic and copies ran while one was open for 4% -> 4% of each run, Pallas kernels for 21% -> 23%
where the time goes in v4:
time: 45.6 us; the launch traced here: 45.3 us
  Pallas kernels  20.1 us (44%)
  starting transfers between devices  16 us (35%)
  waiting for transfers between devices  6.6 us (14%)
  local copies, waits for them, and re-layouts  1.92 us (4%)
  other arithmetic  0.62 us (1%)
    ppermute x15, starting transfers between devices, partner(): lax.ppermute(array, axis, [(i, i ^ k) for i in range(lax.axis_size(axis))])  16 us
    ppermute x15, waiting for transfers between devices, partner(): lax.ppermute(array, axis, [(i, i ^ k) for i in range(lax.axis_size(axis))])  6.6 us
    pallas_call x2, Pallas kernels, fetch(): pl.pallas_call(lambda *refs: fetch_kernel(bounds[n], *refs), out_shape=pi...  6.48 us
    pallas_call x2, Pallas kernels, attend(): pl.pallas_call(lambda *refs: attend_kernel(slots, bounds[n], beams, heads...  5.31 us
    pallas_call x1, Pallas kernels, step(): pl.pallas_call(lambda *refs: project_kernel(ctx_count, far, beams, heads,...  4.71 us
    pallas_call x2, Pallas kernels, near(): pl.pallas_call(lambda *refs: near_kernel(ctx_count, k, beams, bounds, *re...  2.38 us
    transpose x1, local copies, waits for them, and re-layouts, step(): vt = jnp.transpose(cache_values[0], (1, 0, 2))  1.92 us
  transfers between devices with their start and end apart: 15, of which 7 were waited for; matrix products, arithmetic and copies ran while one was open for 4% of the time, Pallas kernels for 23%

profile of v4, /device:TPU:0, one launch (start us, length us, event | category | flops | bytes accessed | tf_op | source)
XLA Modules:
  0.0 45.3 jit_solution(14057139339985866663)
XLA Ops:
  0.0 0.8 %pack.1 = bf16[48,128]{1,0:T(8,128)(2,1)S(1)} custom-call(bf16[1,4096]{1,0:T(2,128)(2,1)} %refs_0_.5, bf16[1,1024]{1,0:T(2,128)(2,1)} %refs_1_.3, bf16[1,1024]{1,0:T(2,128)(2,1)} %refs_2_.3), custom_call_target="tpu_custom_call" | custom-call | tf_op jit(solution)/shard_map/pack/pallas_call | solution.py:265
  0.8 5.1 %collective-permute-start.2 = (bf16[48,128]{1,0:T(8,128)(2,1)S(1)}, bf16[48,128]{1,0:T(8,128)(2,1)S(1)}, u32[]{:S(2)}, u32[]{:S(2)}) collective-permute-start(bf16[48,128]{1,0:T(8,128)(2,1)S(1)} %pack.1), channel_id=1, source_target_pairs={{0,12},{4,8},{8,4},{12,0},{1,13},{5,9},{9,5},{13,1},{2,14},{6,10},... | collective-permute-start | bytes 36872 | tf_op jit(solution)/shard_map/ppermute | solution.py:36
  5.9 0.6 %collective-permute-start = (bf16[48,128]{1,0:T(8,128)(2,1)S(1)}, bf16[48,128]{1,0:T(8,128)(2,1)S(1)}, u32[]{:S(2)}, u32[]{:S(2)}) collective-permute-start(bf16[48,128]{1,0:T(8,128)(2,1)S(1)} %pack.1), channel_id=1, source_target_pairs={{0,4},{4,0},{8,12},{12,8},{1,5},{5,1},{9,13},{13,9},{2,6},{6,2},{1... | collective-permute-start | bytes 36872 | tf_op jit(solution)/shard_map/ppermute | solution.py:36
  6.6 1.0 %collective-permute-done.2 = bf16[48,128]{1,0:T(8,128)(2,1)S(1)} collective-permute-done((bf16[48,128]{1,0:T(8,128)(2,1)S(1)}, bf16[48,128]{1,0:T(8,128)(2,1)S(1)}, u32[]{:S(2)}, u32[]{:S(2)}) %collective-permute-start.2) | collective-permute-done | bytes 12320 | tf_op jit(solution)/shard_map/ppermute | solution.py:36
  7.6 2.9 %collective-permute-done.1 = bf16[48,128]{1,0:T(8,128)(2,1)S(1)} collective-permute-done((bf16[48,128]{1,0:T(8,128)(2,1)S(1)}, bf16[48,128]{1,0:T(8,128)(2,1)S(1)}, u32[]{:S(2)}, u32[]{:S(2)}) %collective-permute-start.1) | collective-permute-done | bytes 12320 | tf_op jit(solution)/shard_map/ppermute | solution.py:36
  10.5 0.1 collective-permute-start.5
  10.6 1.6 %collective-permute-start.4 = (bf16[4,48,128]{2,1,0:T(8,128)(2,1)S(1)}, bf16[4,48,128]{2,1,0:T(8,128)(2,1)S(1)}, u32[]{:S(2)}, u32[]{:S(2)}) collective-permute-start(bf16[4,48,128]{2,1,0:T(8,128)(2,1)S(1)} %pad_maximum_fusion.refs_5_.refs_0_), channel_id=1, source_target_pairs={{0,2},{1,3},{2,0},{3,1},{4,6},{5,7},{6,4},{7,5},{8,10},{9,11},{10,... | collective-permute-start | bytes 147464 | tf_op jit(solution)/shard_map/ppermute | solution.py:36
  12.2 0.3 collective-permute-start.3
  12.5 1.9 %copy_bitcast_fusion = (bf16[8,512,128]{2,1,0:T(8,128)(2,1)S(1)}, bf16[8,512,128]{2,1,0:T(8,128)(2,1)S(1)}) fusion(bf16[1,512,8,128]{3,2,1,0:T(8,128)(2,1)} %param.12, bf16[1,512,8,128]{3,2,1,0:T(8,128)(2,1)} %param.11), kind=kLoop, calls=%fused_computation | loop fusion | bytes 4194304 | tf_op jit(solution)/shard_map/transpose | solution.py:276
  14.4 0.2 collective-permute-done.5.refs_7_
  14.6 0.9 %collective-permute-done.4.refs_6_ = bf16[4,48,128]{2,1,0:T(8,128)(2,1)S(1)} collective-permute-done((bf16[4,48,128]{2,1,0:T(8,128)(2,1)S(1)}, bf16[4,48,128]{2,1,0:T(8,128)(2,1)S(1)}, u32[]{:S(2)}, u32[]{:S(2)}) %collective-permute-start.4) | collective-permute-done | bytes 49184 | tf_op jit(solution)/shard_map/ppermute | solution.py:36
  15.5 2.8 %shard_map.83 = (bf16[144,128]{1,0:T(8,128)(2,1)S(1)}, bf16[144,128]{1,0:T(8,128)(2,1)S(1)}, bf16[144,128]{1,0:T(8,128)(2,1)S(1)}, bf16[640,4096]{1,0:T(8,128)(2,1)S(1)}) custom-call(s32[4]{0:T(128)} %refs_0_.7, s32[4]{0:T(128)} %refs_1_.5, bf16[4096,4096]{1,0:T(8,128)(2,1)} %refs_8_.1, bf16[8,512,128]{2,1,0:T(8,128)(2,1)S(1)} %get-tuple-element.26.refs_3_, ...), custom_call_target="tpu_custom_call" | custom-call | flops 100663296 | bytes 5242880 | tf_op jit(solution)/shard_map/pallas_call | solution.py:255
  18.3 0.2 collective-permute-start.6
  18.5 1.1 %collective-permute-start.7 = (bf16[144,128]{1,0:T(8,128)(2,1)S(1)}, bf16[144,128]{1,0:T(8,128)(2,1)S(1)}, u32[]{:S(2)}, u32[]{:S(2)}) collective-permute-start(bf16[144,128]{1,0:T(8,128)(2,1)S(1)} %get-tuple-element.17), channel_id=1, source_target_pairs={{0,2},{1,3},{2,0},{3,1},{4,6},{5,7},{6,4},{7,5},{8,10},{9,11},{10,... | collective-permute-start | bytes 110600 | tf_op jit(solution)/shard_map/ppermute | solution.py:36
  19.6 0.6 %collective-permute-start.8 = (bf16[144,128]{1,0:T(8,128)(2,1)S(1)}, bf16[144,128]{1,0:T(8,128)(2,1)S(1)}, u32[]{:S(2)}, u32[]{:S(2)}) collective-permute-start(bf16[144,128]{1,0:T(8,128)(2,1)S(1)} %get-tuple-element.18), channel_id=1, source_target_pairs={{0,3},{1,2},{2,1},{3,0},{4,7},{5,6},{6,5},{7,4},{8,11},{9,10},{10,... | collective-permute-start | bytes 110600 | tf_op jit(solution)/shard_map/ppermute | solution.py:36
  20.2 2.5 %shard_map.82 = (bf16[144,128]{1,0:T(8,128)(2,1)S(1)}, bf16[640,4096]{1,0:T(8,128)(2,1)S(1)}) custom-call(s32[4]{0:T(128)} %refs_0_.7, s32[4]{0:T(128)} %refs_1_.5, bf16[4096,4096]{1,0:T(8,128)(2,1)} %refs_8_.1, bf16[8,512,128]{2,1,0:T(8,128)(2,1)S(1)} %get-tuple-element.26.refs_3_, bf16[8,512,128]{2,1,0:T(8,128)(2,1)S(1)} %get-tuple-element.25.refs_4_, ...), custom_call_target="tpu_custom_call" | custom-call | flops 33554432 | bytes 5242880 | tf_op jit(solution)/shard_map/pallas_call | solution.py:255
  22.8 0.0 collective-permute-done.6.refs_2_
  22.8 0.3 collective-permute-done.8.refs_4_
  23.1 0.4 merge.1.refs_0_
  23.5 1.5 %collective-permute-start.11 = (bf16[4,32,128]{2,1,0:T(8,128)(2,1)S(1)}, bf16[4,32,128]{2,1,0:T(8,128)(2,1)S(1)}, u32[]{:S(2)}, u32[]{:S(2)}) collective-permute-start(bf16[4,32,128]{2,1,0:T(8,128)(2,1)S(1)} %merge.1.refs_0_), channel_id=1, source_target_pairs={{0,12},{4,8},{8,4},{12,0},{1,13},{5,9},{9,5},{13,1},{2,14},{6,10},... | collective-permute-start | bytes 98312 | tf_op jit(solution)/shard_map/ppermute | solution.py:36
  25.0 0.6 %collective-permute-start.10 = (bf16[4,32,128]{2,1,0:T(8,128)(2,1)S(1)}, bf16[4,32,128]{2,1,0:T(8,128)(2,1)S(1)}, u32[]{:S(2)}, u32[]{:S(2)}) collective-permute-start(bf16[4,32,128]{2,1,0:T(8,128)(2,1)S(1)} %merge.1.refs_0_), channel_id=1, source_target_pairs={{0,8},{4,12},{8,0},{12,4},{1,9},{5,13},{9,1},{13,5},{2,10},{6,14},... | collective-permute-start | bytes 98312 | tf_op jit(solution)/shard_map/ppermute | solution.py:36
  25.6 2.3 %collective-permute-start.9 = (bf16[4,32,128]{2,1,0:T(8,128)(2,1)S(1)}, bf16[4,32,128]{2,1,0:T(8,128)(2,1)S(1)}, u32[]{:S(2)}, u32[]{:S(2)}) collective-permute-start(bf16[4,32,128]{2,1,0:T(8,128)(2,1)S(1)} %merge.1.refs_0_), channel_id=1, source_target_pairs={{0,4},{4,0},{8,12},{12,8},{1,5},{5,1},{9,13},{13,9},{2,6},{6,2},{1... | collective-permute-start | bytes 98312 | tf_op jit(solution)/shard_map/ppermute | solution.py:36
  27.9 2.5 %shard_map.84.refs_6_.refs_3_ = bf16[640,4096]{1,0:T(8,128)(2,1)S(1)} custom-call(bf16[4096,4096]{1,0:T(8,128)(2,1)} %refs_8_.1), custom_call_target="tpu_custom_call" | custom-call | bytes 5242880 | tf_op jit(solution)/shard_map/pallas_call | solution.py:244
  30.4 4.0 %shard_map.85.refs_7_.refs_4_ = bf16[1280,4096]{1,0:T(8,128)(2,1)S(1)} custom-call(bf16[4096,4096]{1,0:T(8,128)(2,1)} %refs_8_.1), custom_call_target="tpu_custom_call" | custom-call | bytes 10485760 | tf_op jit(solution)/shard_map/pallas_call | solution.py:244
  34.4 4.7 %project.1 = (f32[4,1024]{1,0:T(4,128)S(1)}, f32[4,1024]{1,0:T(4,128)S(1)}, bf16[896,4096]{1,0:T(8,128)(2,1)S(1)}, bf16[8,4096]{1,0:T(8,128)(2,1)S(1)}) custom-call(bf16[4,32,128]{2,1,0:T(8,128)(2,1)S(1)} %merge.1.refs_0_, bf16[4,32,128]{2,1,0:T(8,128)(2,1)S(1)} %collective-permute-done.9.refs_1_, bf16[4,32,128]{2,1,0:T(8,128)(2,1)S(1)} %collective-permute-done.10.refs_2_, ...), custom_call_target="tpu_custom_call" | custom-call | flops 134217728 | bytes 7340032 | tf_op jit(solution)/shard_map/project/pallas_call | solution.py:300
  39.2 1.2 %shard_map.87 = f32[4,1024]{1,0:T(4,128)S(1)} custom-call(bf16[8,4096]{1,0:T(8,128)(2,1)S(1)} %get-tuple-element.21.refs_0_, bf16[640,4096]{1,0:T(8,128)(2,1)S(1)} %get-tuple-element.19.refs_4_.refs_1_, bf16[640,4096]{1,0:T(8,128)(2,1)S(1)} %get-tuple-element.20.refs_5_.refs_2_, bf16[640,4096]{1,0:T(8,128)(2,1)S(1)} %shard_map.84.refs_6_.refs_3_, ...), custom_call_target="tpu_custom_call" | custom-call | flops 67108864 | tf_op jit(solution)/shard_map/pallas_call | solution.py:312
  40.4 1.1 %collective-permute-start.12 = (f32[4,1024]{1,0:T(4,128)S(1)}, f32[4,1024]{1,0:T(4,128)S(1)}, u32[]{:S(2)}, u32[]{:S(2)}) collective-permute-start(f32[4,1024]{1,0:T(4,128)S(1)} %get-tuple-element.23), channel_id=1, source_target_pairs={{0,2},{1,3},{2,0},{3,1},{4,6},{5,7},{6,4},{7,5},{8,10},{9,11},{10,... | collective-permute-start | bytes 49160 | tf_op jit(solution)/shard_map/ppermute | solution.py:36
  41.5 0.7 %collective-permute-start.13 = (f32[4,1024]{1,0:T(4,128)S(1)}, f32[4,1024]{1,0:T(4,128)S(1)}, u32[]{:S(2)}, u32[]{:S(2)}) collective-permute-start(f32[4,1024]{1,0:T(4,128)S(1)} %get-tuple-element.24), channel_id=1, source_target_pairs={{0,3},{1,2},{2,1},{3,0},{4,7},{5,6},{6,5},{7,4},{8,11},{9,10},{10,... | collective-permute-start | bytes 49160 | tf_op jit(solution)/shard_map/ppermute | solution.py:36
  42.2 1.2 %shard_map.86 = f32[4,1024]{1,0:T(4,128)S(1)} custom-call(bf16[8,4096]{1,0:T(8,128)(2,1)S(1)} %get-tuple-element.21.refs_0_, bf16[640,4096]{1,0:T(8,128)(2,1)S(1)} %get-tuple-element.19.refs_4_.refs_1_, bf16[640,4096]{1,0:T(8,128)(2,1)S(1)} %get-tuple-element.20.refs_5_.refs_2_, bf16[640,4096]{1,0:T(8,128)(2,1)S(1)} %shard_map.84.refs_6_.refs_3_, ...), custom_call_target="tpu_custom_call" | custom-call | flops 67108864 | tf_op jit(solution)/shard_map/pallas_call | solution.py:312
  43.4 0.7 %collective-permute-done.12 = f32[4,1024]{1,0:T(4,128)S(1)} collective-permute-done((f32[4,1024]{1,0:T(4,128)S(1)}, f32[4,1024]{1,0:T(4,128)S(1)}, u32[]{:S(2)}, u32[]{:S(2)}) %collective-permute-start.12) | collective-permute-done | bytes 16416 | tf_op jit(solution)/shard_map/ppermute | solution.py:36
  44.1 0.5 %collective-permute-done.13 = f32[4,1024]{1,0:T(4,128)S(1)} collective-permute-done((f32[4,1024]{1,0:T(4,128)S(1)}, f32[4,1024]{1,0:T(4,128)S(1)}, u32[]{:S(2)}, u32[]{:S(2)}) %collective-permute-start.13) | collective-permute-done | bytes 16416 | tf_op jit(solution)/shard_map/ppermute | solution.py:36
  44.7 0.6 %add_convert_fusion = bf16[4,1024]{1,0:T(4,128)(2,1)} fusion(f32[4,1024]{1,0:T(4,128)S(1)} %collective-permute-done.14, f32[4,1024]{1,0:T(4,128)S(1)} %collective-permute-done.13, f32[4,1024]{1,0:T(4,128)S(1)} %shard_map.86, f32[4,1024]{1,0:T(4,128)S(1)} %collective-permute-done.12), kind=kLoop, calls=%fused_computation.3 | loop fusion | flops 16384 | bytes 73728 | tf_op jit(solution)/shard_map/convert_element_type | solution.py:327
  (10 shorter events, 0.0 us)
Async XLA Ops:
  0.8 6.8 %collective-permute-start.2 = (bf16[48,128]{1,0:T(8,128)(2,1)S(1)}, bf16[48,128]{1,0:T(8,128)(2,1)S(1)}, u32[]{:S(2)}, u32[]{:S(2)}) collective-permute-start(bf16[48,128]{1,0:T(8,128)(2,1)S(1)} %pack.1), channel_id=1, source_target_pairs={{0,12},{4,8},{8,4},{12,0},{1,13},{5,9},{9,5},{13,1},{2,14},{6,10},... | collective-permute-start | bytes 36872 | tf_op jit(solution)/shard_map/ppermute | solution.py:36
  5.9 4.6 %collective-permute-start.1 = (bf16[48,128]{1,0:T(8,128)(2,1)S(1)}, bf16[48,128]{1,0:T(8,128)(2,1)S(1)}, u32[]{:S(2)}, u32[]{:S(2)}) collective-permute-start(bf16[48,128]{1,0:T(8,128)(2,1)S(1)} %pack.1), channel_id=1, source_target_pairs={{0,8},{4,12},{8,0},{12,4},{1,9},{5,13},{9,1},{13,5},{2,10},{6,14},... | collective-permute-start | bytes 36872 | tf_op jit(solution)/shard_map/ppermute | solution.py:36
  5.9 4.6 %collective-permute-start = (bf16[48,128]{1,0:T(8,128)(2,1)S(1)}, bf16[48,128]{1,0:T(8,128)(2,1)S(1)}, u32[]{:S(2)}, u32[]{:S(2)}) collective-permute-start(bf16[48,128]{1,0:T(8,128)(2,1)S(1)} %pack.1), channel_id=1, source_target_pairs={{0,4},{4,0},{8,12},{12,8},{1,5},{5,1},{9,13},{13,9},{2,6},{6,2},{1... | collective-permute-start | bytes 36872 | tf_op jit(solution)/shard_map/ppermute | solution.py:36
  10.5 4.0 %collective-permute-start.5 = (bf16[4,48,128]{2,1,0:T(8,128)(2,1)S(1)}, bf16[4,48,128]{2,1,0:T(8,128)(2,1)S(1)}, u32[]{:S(2)}, u32[]{:S(2)}) collective-permute-start(bf16[4,48,128]{2,1,0:T(8,128)(2,1)S(1)} %pad_maximum_fusion.refs_5_.refs_0_), channel_id=1, source_target_pairs={{0,3},{1,2},{2,1},{3,0},{4,7},{5,6},{6,5},{7,4},{8,11},{9,10},{10,... | collective-permute-start | bytes 147464 | tf_op jit(solution)/shard_map/ppermute | solution.py:36
  10.6 4.9 %collective-permute-start.4 = (bf16[4,48,128]{2,1,0:T(8,128)(2,1)S(1)}, bf16[4,48,128]{2,1,0:T(8,128)(2,1)S(1)}, u32[]{:S(2)}, u32[]{:S(2)}) collective-permute-start(bf16[4,48,128]{2,1,0:T(8,128)(2,1)S(1)} %pad_maximum_fusion.refs_5_.refs_0_), channel_id=1, source_target_pairs={{0,2},{1,3},{2,0},{3,1},{4,6},{5,7},{6,4},{7,5},{8,10},{9,11},{10,... | collective-permute-start | bytes 147464 | tf_op jit(solution)/shard_map/ppermute | solution.py:36
  12.2 3.3 %collective-permute-start.3 = (bf16[4,48,128]{2,1,0:T(8,128)(2,1)S(1)}, bf16[4,48,128]{2,1,0:T(8,128)(2,1)S(1)}, u32[]{:S(2)}, u32[]{:S(2)}) collective-permute-start(bf16[4,48,128]{2,1,0:T(8,128)(2,1)S(1)} %pad_maximum_fusion.refs_5_.refs_0_), channel_id=1, source_target_pairs={{0,1},{1,0},{2,3},{3,2},{4,5},{5,4},{6,7},{7,6},{8,9},{9,8},{10,11... | collective-permute-start | bytes 147464 | tf_op jit(solution)/shard_map/ppermute | solution.py:36
  18.3 4.5 %collective-permute-start.6 = (bf16[144,128]{1,0:T(8,128)(2,1)S(1)}, bf16[144,128]{1,0:T(8,128)(2,1)S(1)}, u32[]{:S(2)}, u32[]{:S(2)}) collective-permute-start(bf16[144,128]{1,0:T(8,128)(2,1)S(1)} %get-tuple-element.16), channel_id=1, source_target_pairs={{0,1},{1,0},{2,3},{3,2},{4,5},{5,4},{6,7},{7,6},{8,9},{9,8},{10,11... | collective-permute-start | bytes 110600 | tf_op jit(solution)/shard_map/ppermute | solution.py:36
  18.5 4.3 %collective-permute-start.7 = (bf16[144,128]{1,0:T(8,128)(2,1)S(1)}, bf16[144,128]{1,0:T(8,128)(2,1)S(1)}, u32[]{:S(2)}, u32[]{:S(2)}) collective-permute-start(bf16[144,128]{1,0:T(8,128)(2,1)S(1)} %get-tuple-element.17), channel_id=1, source_target_pairs={{0,2},{1,3},{2,0},{3,1},{4,6},{5,7},{6,4},{7,5},{8,10},{9,11},{10,... | collective-permute-start | bytes 110600 | tf_op jit(solution)/shard_map/ppermute | solution.py:36
  19.6 3.4 %collective-permute-start.8 = (bf16[144,128]{1,0:T(8,128)(2,1)S(1)}, bf16[144,128]{1,0:T(8,128)(2,1)S(1)}, u32[]{:S(2)}, u32[]{:S(2)}) collective-permute-start(bf16[144,128]{1,0:T(8,128)(2,1)S(1)} %get-tuple-element.18), channel_id=1, source_target_pairs={{0,3},{1,2},{2,1},{3,0},{4,7},{5,6},{6,5},{7,4},{8,11},{9,10},{10,... | collective-permute-start | bytes 110600 | tf_op jit(solution)/shard_map/ppermute | solution.py:36
  23.5 11.0 %collective-permute-start.11 = (bf16[4,32,128]{2,1,0:T(8,128)(2,1)S(1)}, bf16[4,32,128]{2,1,0:T(8,128)(2,1)S(1)}, u32[]{:S(2)}, u32[]{:S(2)}) collective-permute-start(bf16[4,32,128]{2,1,0:T(8,128)(2,1)S(1)} %merge.1.refs_0_), channel_id=1, source_target_pairs={{0,12},{4,8},{8,4},{12,0},{1,13},{5,9},{9,5},{13,1},{2,14},{6,10},... | collective-permute-start | bytes 98312 | tf_op jit(solution)/shard_map/ppermute | solution.py:36
  25.0 9.4 %collective-permute-start.10 = (bf16[4,32,128]{2,1,0:T(8,128)(2,1)S(1)}, bf16[4,32,128]{2,1,0:T(8,128)(2,1)S(1)}, u32[]{:S(2)}, u32[]{:S(2)}) collective-permute-start(bf16[4,32,128]{2,1,0:T(8,128)(2,1)S(1)} %merge.1.refs_0_), channel_id=1, source_target_pairs={{0,8},{4,12},{8,0},{12,4},{1,9},{5,13},{9,1},{13,5},{2,10},{6,14},... | collective-permute-start | bytes 98312 | tf_op jit(solution)/shard_map/ppermute | solution.py:36
  25.6 8.8 %collective-permute-start.9 = (bf16[4,32,128]{2,1,0:T(8,128)(2,1)S(1)}, bf16[4,32,128]{2,1,0:T(8,128)(2,1)S(1)}, u32[]{:S(2)}, u32[]{:S(2)}) collective-permute-start(bf16[4,32,128]{2,1,0:T(8,128)(2,1)S(1)} %merge.1.refs_0_), channel_id=1, source_target_pairs={{0,4},{4,0},{8,12},{12,8},{1,5},{5,1},{9,13},{13,9},{2,6},{6,2},{1... | collective-permute-start | bytes 98312 | tf_op jit(solution)/shard_map/ppermute | solution.py:36
  40.4 3.1 %collective-permute-start.14 = (f32[4,1024]{1,0:T(4,128)S(1)}, f32[4,1024]{1,0:T(4,128)S(1)}, u32[]{:S(2)}, u32[]{:S(2)}) collective-permute-start(f32[4,1024]{1,0:T(4,128)S(1)} %shard_map.87), channel_id=1, source_target_pairs={{0,1},{1,0},{2,3},{3,2},{4,5},{5,4},{6,7},{7,6},{8,9},{9,8},{10,11... | collective-permute-start | bytes 49160 | tf_op jit(solution)/shard_map/ppermute | solution.py:36
  40.4 3.8 %collective-permute-start.12 = (f32[4,1024]{1,0:T(4,128)S(1)}, f32[4,1024]{1,0:T(4,128)S(1)}, u32[]{:S(2)}, u32[]{:S(2)}) collective-permute-start(f32[4,1024]{1,0:T(4,128)S(1)} %get-tuple-element.23), channel_id=1, source_target_pairs={{0,2},{1,3},{2,0},{3,1},{4,6},{5,7},{6,4},{7,5},{8,10},{9,11},{10,... | collective-permute-start | bytes 49160 | tf_op jit(solution)/shard_map/ppermute | solution.py:36
  41.5 3.2 %collective-permute-start.13 = (f32[4,1024]{1,0:T(4,128)S(1)}, f32[4,1024]{1,0:T(4,128)S(1)}, u32[]{:S(2)}, u32[]{:S(2)}) collective-permute-start(f32[4,1024]{1,0:T(4,128)S(1)} %get-tuple-element.24), channel_id=1, source_target_pairs={{0,3},{1,2},{2,1},{3,0},{4,7},{5,6},{6,5},{7,4},{8,11},{9,10},{10,... | collective-permute-start | bytes 49160 | tf_op jit(solution)/shard_map/ppermute | solution.py:36
